TPU v7x, 32 devices: a whole 2x2x4 slice. The times are simulated.
32 devices in a mesh: wide: 4 (over z), narrow: 8 (over y, x, core).
Axes of the slice: x: 2, y: 2, z: 4, core: 2. Of those that a mesh axis runs over, the one named last changes fastest.
Arguments:
- samples: bfloat16 [1024, 2, 102144], P(('wide', 'narrow')), may hold values from -6 to 6
- filter_taps: float32 [16, 256], replicated, may hold values from -1.5 to 1.5
- beam_weights: bfloat16 [256, 2, 2, 512, 1024], P(('narrow', 'wide')), may hold values from -0.1875 to 0.1875
- smooth_kernel: float32 [33, 33], replicated, may hold values from -0.1875 to 0.1875
Outputs:
- detection: float32 [256, 48, 1024], P('narrow', None, 'wide')
All inputs are finite; a program needn't handle non-finite values.
Results may differ from a plain program's by a relative error of at most 0.012.
The roundings to bfloat16 on the way count: a program that leaves them out, or rounds other values in their place, can miss the bound.
Values may be sent and summed in bfloat16 or wider, within the bound.
A program may use at most 320 MiB of HBM per device.

v0:
```python
import functools

import jax
import jax.numpy as jnp
from jax import lax
from jax.experimental import pallas as pl
from jax.experimental.pallas import tpu as pltpu
from jax.sharding import PartitionSpec as P

INTEG = 8
HALF = 16
LANES = 128
PORTION = 128
BAND = 8


def with_halo(block, sides, width):
    for axis, dim in sides:
        count = lax.axis_size(axis)
        forward = [(i, i + 1) for i in range(count - 1)]
        backward = [(target, source) for source, target in forward]
        low = lax.ppermute(
            lax.slice_in_dim(block, block.shape[dim] - width, None, axis=dim), axis, forward
        )
        high = lax.ppermute(lax.slice_in_dim(block, 0, width, axis=dim), axis, backward)
        block = jnp.concatenate([low, block, high], axis=dim)
    return block


def fourier_rows(points, owner_of):
    column = jnp.arange(points, dtype=jnp.int32)
    channel = owner_of(column)
    phase_index = channel[:, None] * column[None, :] % points
    angles = phase_index.astype(jnp.float32) * jnp.float32(2.0 * jnp.pi / points)
    scale = jnp.float32(1.0 / points**0.5)
    cosine = jnp.cos(angles) * scale
    sine_part = jnp.sin(angles) * scale
    real_row = jnp.stack([cosine, sine_part], axis=1)
    imag_row = jnp.stack([-sine_part, cosine], axis=1)
    return jnp.stack([real_row, imag_row], axis=1).reshape(2 * points, 2 * points)


def split(value):
    high = value.astype(jnp.bfloat16)
    return high, (value - high.astype(jnp.float32)).astype(jnp.bfloat16)


def channelize_kernel(
    taps_ref, table_ref, main_ref, halo_ref, out_ref, window_ref, high_ref, low_ref, turned_ref
):
    tap_count, points = taps_ref.shape
    group = main_ref.shape[1]
    spectra = main_ref.shape[2] // points
    high_ref[...], low_ref[...] = split(table_ref[...])
    blocks = spectra // tap_count

    for part in range(2):
        for tile in range(points // LANES):
            lane = tile * LANES
            column = part * (points // LANES) + tile
            for base in range(0, group, 8):
                coeffs = [
                    jnp.broadcast_to(taps_ref[tap : tap + 1, lane : lane + LANES], (8, LANES))
                    for tap in range(tap_count)
                ]

                def load(ref, frame):
                    start = pl.multiple_of(frame * points + lane, LANES)
                    rows = ref[part, base : base + 8, pl.ds(start, LANES)]
                    return rows.astype(jnp.float32)

                def emit(block, older, newer_ref, newer_base):
                    sums = list(older)
                    nexts = [None] * tap_count
                    for step in range(tap_count):
                        value = load(newer_ref, newer_base + step)
                        for index in range(tap_count):
                            tap = tap_count + step - index
                            if tap < tap_count:
                                sums[index] = sums[index] + coeffs[tap] * value
                            tap = step - index
                            if 0 <= tap:
                                term = coeffs[tap] * value
                                nexts[index] = (
                                    term if nexts[index] is None else nexts[index] + term
                                )
                        window_ref[
                            column,
                            pl.ds(base * spectra + block * tap_count + step, 8, stride=spectra),
                            :,
                        ] = sums[step]
                    return tuple(nexts)

                first = [None] * tap_count
                for step in range(tap_count):
                    value = load(main_ref, step)
                    for index in range(step + 1):
                        term = coeffs[step - index] * value
                        first[index] = term if first[index] is None else first[index] + term

                def body(block, older):
                    return emit(block, older, main_ref, (block + 1) * tap_count)

                older = lax.fori_loop(0, blocks - 1, body, tuple(first))
                sums = list(older)
                window_ref[
                    column,
                    pl.ds(base * spectra + (blocks - 1) * tap_count, 8, stride=spectra),
                    :,
                ] = sums[0]
                for step in range(tap_count - 1):
                    value = load(halo_ref, step)
                    for index in range(step + 1, tap_count):
                        sums[index] = sums[index] + coeffs[tap_count + step - index] * value
                    window_ref[
                        column,
                        pl.ds(
                            base * spectra + (blocks - 1) * tap_count + step + 1, 8, stride=spectra
                        ),
                        :,
                    ] = sums[step + 1]

    columns = window_ref.shape[0]
    contract = (((1,), (1,)), ((), ()))

    @pl.loop(0, group)
    def _(index):
        rows = pl.ds(pl.multiple_of(index * spectra, spectra), spectra)
        signal = jnp.concatenate([window_ref[column, rows, :] for column in range(columns)], axis=1)
        high, low = split(signal)
        product = functools.partial(
            lax.dot_general, dimension_numbers=contract, preferred_element_type=jnp.float32
        )
        result = (
            product(low_ref[...], high) + product(high_ref[...], low) + product(high_ref[...], high)
        )
        turned_ref[pl.ds(index, result.shape[0], stride=group), :] = result

    out_ref[...] = turned_ref[...].reshape(out_ref.shape).astype(out_ref.dtype)


def channelize(by_part, filter_taps, table, portion):
    tap_count, points = filter_taps.shape
    inputs_here = by_part.shape[1]
    group = min(16, inputs_here)
    rows = table.shape[0]
    halo = tap_count * points
    return pl.pallas_call(
        channelize_kernel,
        grid=(inputs_here // group,),
        in_specs=[
            pl.BlockSpec(filter_taps.shape, lambda g: (0, 0)),
            pl.BlockSpec(table.shape, lambda g: (0, 0)),
            pl.BlockSpec((2, group, PORTION * points), lambda g: (0, g, portion)),
            pl.BlockSpec(
                (2, group, halo), lambda g: (0, g, (portion + 1) * (PORTION // tap_count))
            ),
        ],
        out_specs=pl.BlockSpec((rows, group, PORTION), lambda g: (0, g, 0)),
        out_shape=jax.ShapeDtypeStruct((rows, inputs_here, PORTION), jnp.bfloat16),
        scratch_shapes=[
            pltpu.VMEM((2 * points // LANES, group * PORTION, LANES), jnp.float32),
            pltpu.VMEM(table.shape, jnp.bfloat16),
            pltpu.VMEM(table.shape, jnp.bfloat16),
            pltpu.VMEM((rows * group, PORTION), jnp.float32),
        ],
        cost_estimate=pl.CostEstimate(
            flops=6 * rows * rows * inputs_here * PORTION,
            bytes_accessed=8 * inputs_here * points * PORTION,
            transcendentals=0,
        ),
        compiler_params=pltpu.CompilerParams(vmem_limit_bytes=48 * 1024 * 1024),
        name=f"channelize_{portion}",
    )(filter_taps, table, by_part, by_part)


def beam_kernel(voltage_ref, weight_ref, out_ref):
    sources, _, inputs_each, spectra = voltage_ref.shape
    pols, _, dishes, beams = weight_ref.shape[1:]
    per_pol = sources // pols

    def dish_rows(pol, part):
        rows = voltage_ref[pol * per_pol : (pol + 1) * per_pol, part]
        if inputs_each % 16 != 0:
            rows = rows.astype(jnp.float32)
        return rows.reshape(dishes, spectra).astype(jnp.float32).T.astype(jnp.bfloat16)

    energy = None
    for pol in range(pols):
        real = dish_rows(pol, 0)
        imag = dish_rows(pol, 1)
        left = jnp.concatenate(
            [jnp.concatenate([real, -imag], axis=1), jnp.concatenate([imag, real], axis=1)], axis=0
        )
        weights = weight_ref[0, pol].reshape(2 * dishes, beams)
        formed = jnp.dot(left, weights, preferred_element_type=jnp.float32)
        squares = formed * formed
        power = squares[:spectra] + squares[spectra:]
        energy = power if energy is None else energy + power
    binned = energy.reshape(spectra // INTEG, INTEG, beams).sum(axis=1)
    intensity = (binned * jnp.float32(1.0 / (pols * INTEG))).astype(jnp.bfloat16)
    share = out_ref.shape[3]
    for owner in range(out_ref.shape[0]):
        out_ref[owner, 0] = intensity[:, owner * share : (owner + 1) * share]


def beam_power(turned, beam_weights, portion, owners):
    sources, rows, inputs_each, spectra = turned.shape
    per_device, pols, _, dishes, beams = beam_weights.shape
    return pl.pallas_call(
        beam_kernel,
        grid=(per_device,),
        in_specs=[
            pl.BlockSpec((sources, 2, inputs_each, spectra), lambda c: (0, c, 0, 0)),
            pl.BlockSpec((1, pols, 2, dishes, beams), lambda c: (c, 0, 0, 0, 0)),
        ],
        out_specs=pl.BlockSpec(
            (owners, 1, spectra // INTEG, beams // owners), lambda c: (0, c, 0, 0)
        ),
        out_shape=jax.ShapeDtypeStruct(
            (owners, per_device, spectra // INTEG, beams // owners), jnp.bfloat16
        ),
        cost_estimate=pl.CostEstimate(
            flops=16 * per_device * dishes * spectra * beams,
            bytes_accessed=2 * beam_weights.size + 2 * turned.size,
            transcendentals=0,
        ),
        compiler_params=pltpu.CompilerParams(vmem_limit_bytes=48 * 1024 * 1024),
        name=f"beams_{portion}",
    )(turned, beam_weights)


def band_matrix(smooth_kernel, bin_count):
    extent = smooth_kernel.shape[0]
    half_width = extent // 2
    span = BAND + extent - 1
    offsets = jnp.arange(extent, dtype=jnp.int32)
    bins = jnp.arange(bin_count, dtype=jnp.int32)
    distance = bins[None, :] - bins[:, None] + half_width
    in_time = (distance[None] == offsets[:, None, None]).astype(jnp.float32)
    steps = jnp.arange(span, dtype=jnp.int32)[None, :] - jnp.arange(BAND, dtype=jnp.int32)[:, None]
    in_band = (steps[None] == offsets[:, None, None]).astype(jnp.float32)
    rows = jnp.einsum("kcj,kd->cjd", in_band, smooth_kernel, precision=lax.Precision.HIGHEST)
    matrix = jnp.einsum("cjd,dtu->ctju", rows, in_time, precision=lax.Precision.HIGHEST)
    return matrix.reshape(BAND * bin_count, span * bin_count)


def smooth(extended, matrix, half_width):
    channels_here = extended.shape[0] - 2 * half_width
    bin_count, beams = extended.shape[1:]
    values = extended.astype(jnp.float32)
    centered = values - jnp.mean(values, axis=1, keepdims=True)
    flat = centered.reshape(-1, beams)
    pieces = []
    for start in range(0, channels_here, BAND):
        rows = lax.slice_in_dim(flat, start * bin_count, start * bin_count + matrix.shape[1], axis=0)
        pieces.append(
            jnp.dot(
                matrix, rows, precision=lax.Precision.HIGH, preferred_element_type=jnp.float32
            )
        )
    return jnp.concatenate(pieces, axis=0).reshape(channels_here, bin_count, beams)


def body(samples, filter_taps, beam_weights, smooth_kernel):
    tap_count, points = filter_taps.shape
    wide_count = lax.axis_size("wide")
    narrow_count = lax.axis_size("narrow")
    devices = wide_count * narrow_count
    per_device = points // devices

    def owner_of(column):
        device_slot = column // per_device
        return (
            device_slot % narrow_count * wide_count + device_slot // narrow_count
        ) * per_device + column % per_device

    table = fourier_rows(points, owner_of)
    frames = samples.shape[2] // points
    spectra = frames - tap_count + 1
    by_part = jnp.transpose(samples, (1, 0, 2))
    matrix = band_matrix(smooth_kernel, spectra // INTEG)
    turned = []
    for portion in range(spectra // PORTION):
        voltage = channelize(by_part, filter_taps, table, portion)
        arranged = voltage.reshape(devices, 2 * per_device, -1, PORTION)
        turned.append(
            lax.all_to_all(arranged, ("wide", "narrow"), split_axis=0, concat_axis=0, tiled=True)
        )
    pieces = [
        beam_power(block, beam_weights, portion, wide_count)
        for portion, block in enumerate(turned)
    ]
    intensity = jnp.concatenate(pieces, axis=2)
    by_beam = lax.all_to_all(intensity, "wide", split_axis=0, concat_axis=0, tiled=True)
    by_beam = by_beam.reshape(-1, *by_beam.shape[2:])
    half_width = smooth_kernel.shape[0] // 2
    extended = with_halo(by_beam, (("narrow", 0),), half_width)
    return smooth(extended, matrix, half_width)


def solution(mesh):
    placed = (
        P(("wide", "narrow"), None, None),
        P(),
        P(("narrow", "wide"), None, None, None, None),
        P(),
    )
    return jax.shard_map(
        body, mesh=mesh, in_specs=placed, out_specs=P("narrow", None, "wide"), check_vma=False
    )
```

profile of v0, /device:TPU:4, one launch (start us, length us, event | category | flops | bytes accessed | tf_op | source)
XLA Modules:
  0.0 419.0 jit_solution(8642495716528268842)
XLA Ops:
  2.2 11.8 %copy.16 = bf16[32,2,102144]{2,0,1:T(8,128)(2,1)} copy(bf16[32,2,102144]{2,1,0:T(2,128)(2,1)} %param.4) | data formatting | bytes 26148864 | tf_op args[0]
  14.0 34.1 %channelize_0.1 = bf16[512,32,128]{2,1,0:T(8,128)(2,1)S(1)} custom-call(f32[16,256]{1,0:T(8,128)S(1)} %copy-done.4, f32[512,512]{1,0:T(8,128)S(1)} %bitcast.44, bf16[2,32,102144]{2,1,0:T(8,128)(2,1)} %bitcast.50, bf16[2,32,102144]{2,1,0:T(8,128)(2,1)} %bitcast.51), custom_call_target="tpu_custom_call" | custom-call | flops 6442450944 | bytes 8388608 | tf_op jit(solution)/shard_map/channelize_0/pallas_call | solution.py:148
  48.1 2.0 copy-done.3
  50.1 6.2 %all-to-all-start = ((bf16[32,16,32,128]{3,2,1,0:T(8,128)(2,1)}), bf16[32,16,32,128]{3,2,1,0:T(8,128)(2,1)}, u32[]{:S(2)}, u32[]{:S(2)}) async-start(bf16[32,16,32,128]{3,2,1,0:T(8,128)(2,1)} %bitcast.49), calls=%async_computation | async-start | bytes 8388608 | tf_op jit(solution)/shard_map/all_to_all | solution.py:288
  56.2 34.1 %channelize_1.1 = bf16[512,32,128]{2,1,0:T(8,128)(2,1)S(1)} custom-call(f32[16,256]{1,0:T(8,128)S(1)} %copy-done.4, f32[512,512]{1,0:T(8,128)S(1)} %bitcast.45, bf16[2,32,102144]{2,1,0:T(8,128)(2,1)} %bitcast.52, bf16[2,32,102144]{2,1,0:T(8,128)(2,1)} %bitcast.53), custom_call_target="tpu_custom_call" | custom-call | flops 6442450944 | bytes 8388608 | tf_op jit(solution)/shard_map/channelize_1/pallas_call | solution.py:148
  90.4 2.0 copy-done.2
  92.4 57.3 %all-to-all-done.voltage_ref = bf16[32,16,32,128]{3,2,1,0:T(8,128)(2,1)} async-done(((bf16[32,16,32,128]{3,2,1,0:T(8,128)(2,1)}), bf16[32,16,32,128]{3,2,1,0:T(8,128)(2,1)}, u32[]{:S(2)}, u32[]{:S(2)}) %all-to-all-start) | async-done | bytes 4194336 | tf_op jit(solution)/shard_map/all_to_all | solution.py:288
  149.6 4.5 %all-to-all-start.1 = ((bf16[32,16,32,128]{3,2,1,0:T(8,128)(2,1)}), bf16[32,16,32,128]{3,2,1,0:T(8,128)(2,1)}, u32[]{:S(2)}, u32[]{:S(2)}) async-start(bf16[32,16,32,128]{3,2,1,0:T(8,128)(2,1)} %bitcast.48), calls=%async_computation.1 | async-start | bytes 8388608 | tf_op jit(solution)/shard_map/all_to_all | solution.py:288
  154.2 34.1 %channelize_2.1 = bf16[512,32,128]{2,1,0:T(8,128)(2,1)S(1)} custom-call(f32[16,256]{1,0:T(8,128)S(1)} %copy-done.4, f32[512,512]{1,0:T(8,128)S(1)} %bitcast.46, bf16[2,32,102144]{2,1,0:T(8,128)(2,1)} %bitcast.54, bf16[2,32,102144]{2,1,0:T(8,128)(2,1)} %bitcast.55), custom_call_target="tpu_custom_call" | custom-call | flops 6442450944 | bytes 8388608 | tf_op jit(solution)/shard_map/channelize_2/pallas_call | solution.py:148
  188.3 1.9 copy-done.1
  190.3 57.3 %all-to-all-done.1.voltage_ref = bf16[32,16,32,128]{3,2,1,0:T(8,128)(2,1)} async-done(((bf16[32,16,32,128]{3,2,1,0:T(8,128)(2,1)}), bf16[32,16,32,128]{3,2,1,0:T(8,128)(2,1)}, u32[]{:S(2)}, u32[]{:S(2)}) %all-to-all-start.1) | async-done | bytes 4194336 | tf_op jit(solution)/shard_map/all_to_all | solution.py:288
  247.6 4.5 %all-to-all-start.2 = ((bf16[32,16,32,128]{3,2,1,0:T(8,128)(2,1)}), bf16[32,16,32,128]{3,2,1,0:T(8,128)(2,1)}, u32[]{:S(2)}, u32[]{:S(2)}) async-start(bf16[32,16,32,128]{3,2,1,0:T(8,128)(2,1)} %bitcast.47), calls=%async_computation.2 | async-start | bytes 8388608 | tf_op jit(solution)/shard_map/all_to_all | solution.py:288
  252.1 17.5 %beams_0.1 = bf16[4,8,16,256]{3,2,1,0:T(8,128)(2,1)S(1)} custom-call(bf16[32,16,32,128]{3,2,1,0:T(8,128)(2,1)} %all-to-all-done.voltage_ref, bf16[8,2,2,512,1024]{4,3,2,1,0:T(8,128)(2,1)} %weight_ref.5), custom_call_target="tpu_custom_call" | custom-call | flops 8589934592 | bytes 37748736 | tf_op jit(solution)/shard_map/beams_0/pallas_call | solution.py:210
  269.6 17.5 %beams_1.1 = bf16[4,8,16,256]{3,2,1,0:T(8,128)(2,1)S(1)} custom-call(bf16[32,16,32,128]{3,2,1,0:T(8,128)(2,1)} %all-to-all-done.1.voltage_ref, bf16[8,2,2,512,1024]{4,3,2,1,0:T(8,128)(2,1)} %weight_ref.5), custom_call_target="tpu_custom_call" | custom-call | flops 8589934592 | bytes 37748736 | tf_op jit(solution)/shard_map/beams_1/pallas_call | solution.py:210
  287.1 58.4 %all-to-all-done.2.voltage_ref = bf16[32,16,32,128]{3,2,1,0:T(8,128)(2,1)} async-done(((bf16[32,16,32,128]{3,2,1,0:T(8,128)(2,1)}), bf16[32,16,32,128]{3,2,1,0:T(8,128)(2,1)}, u32[]{:S(2)}, u32[]{:S(2)}) %all-to-all-start.2) | async-done | bytes 4194336 | tf_op jit(solution)/shard_map/all_to_all | solution.py:288
  345.5 17.5 %beams_2.1 = bf16[4,8,16,256]{3,2,1,0:T(8,128)(2,1)S(1)} custom-call(bf16[32,16,32,128]{3,2,1,0:T(8,128)(2,1)} %all-to-all-done.2.voltage_ref, bf16[8,2,2,512,1024]{4,3,2,1,0:T(8,128)(2,1)} %weight_ref.5), custom_call_target="tpu_custom_call" | custom-call | flops 8589934592 | bytes 37748736 | tf_op jit(solution)/shard_map/beams_2/pallas_call | solution.py:210
  363.9 3.5 all-to-all-start.3
  367.8 19.7 %all-to-all-done.3 = bf16[4,8,48,256]{3,2,1,0:T(8,128)(2,1)S(1)} async-done(((bf16[4,8,48,256]{3,2,1,0:T(8,128)(2,1)}), bf16[4,8,48,256]{3,2,1,0:T(8,128)(2,1)S(1)}, u32[]{:S(2)}, u32[]{:S(2)}) %all-to-all-start.3) | async-done | bytes 786464 | tf_op jit(solution)/shard_map/all_to_all | solution.py:295
  388.6 1.9 collective-permute-start
  390.5 4.5 %collective-permute-start.1 = (bf16[16,48,256]{2,1,0:T(8,128)(2,1)}, bf16[16,48,256]{2,1,0:T(8,128)(2,1)}, u32[]{:S(2)}, u32[]{:S(2)}) collective-permute-start(bf16[16,48,256]{2,1,0:T(8,128)(2,1)} %bitcast.13), channel_id=1, source_target_pairs={{1,0},{2,1},{3,2},{4,3},{5,4},{6,5},{7,6},{9,8},{10,9},{11,10},{12... | collective-permute-start | bytes 1179656 | tf_op jit(solution)/shard_map/ppermute | solution.py:25
  395.0 3.3 convolution_bitcast_fusion
  398.3 3.6 copy.10
  401.9 5.7 %reshape.230 = f32[384,1920]{1,0:T(8,128)S(1)} reshape(f32[8,48,40,48]{3,2,1,0:T(8,128)} %copy.10) | data formatting | bytes 5898240 | tf_op jit(solution)/shard_map/reshape | solution.py:245
  407.6 1.7 convert_reduce_fusion
  (32 shorter events, 14.1 us)
Async XLA Ops:
  0.0 367.5 %copy-start = (f32[33,33]{1,0:T(8,128)S(1)}, f32[33,33]{1,0:T(8,128)}, u32[]{:S(2)}) copy-start(f32[33,33]{1,0:T(8,128)} %param.7) | copy-start | bytes 13072
  2.2 11.8 %copy-start.4 = (f32[16,256]{1,0:T(8,128)S(1)}, f32[16,256]{1,0:T(8,128)}, u32[]{:S(2)}) copy-start(f32[16,256]{1,0:T(8,128)} %taps_ref.5) | copy-start | bytes 49156
  48.1 2.0 copy-start.3
  50.1 99.6 %all-to-all-start = ((bf16[32,16,32,128]{3,2,1,0:T(8,128)(2,1)}), bf16[32,16,32,128]{3,2,1,0:T(8,128)(2,1)}, u32[]{:S(2)}, u32[]{:S(2)}) async-start(bf16[32,16,32,128]{3,2,1,0:T(8,128)(2,1)} %bitcast.49), calls=%async_computation | async-start | bytes 8388608 | tf_op jit(solution)/shard_map/all_to_all | solution.py:288
  90.3 2.0 copy-start.2
  149.6 97.9 %all-to-all-start.1 = ((bf16[32,16,32,128]{3,2,1,0:T(8,128)(2,1)}), bf16[32,16,32,128]{3,2,1,0:T(8,128)(2,1)}, u32[]{:S(2)}, u32[]{:S(2)}) async-start(bf16[32,16,32,128]{3,2,1,0:T(8,128)(2,1)} %bitcast.48), calls=%async_computation.1 | async-start | bytes 8388608 | tf_op jit(solution)/shard_map/all_to_all | solution.py:288
  188.3 2.0 copy-start.1
  247.6 97.9 %all-to-all-start.2 = ((bf16[32,16,32,128]{3,2,1,0:T(8,128)(2,1)}), bf16[32,16,32,128]{3,2,1,0:T(8,128)(2,1)}, u32[]{:S(2)}, u32[]{:S(2)}) async-start(bf16[32,16,32,128]{3,2,1,0:T(8,128)(2,1)} %bitcast.47), calls=%async_computation.2 | async-start | bytes 8388608 | tf_op jit(solution)/shard_map/all_to_all | solution.py:288
  363.9 23.6 %all-to-all-start.3 = ((bf16[4,8,48,256]{3,2,1,0:T(8,128)(2,1)}), bf16[4,8,48,256]{3,2,1,0:T(8,128)(2,1)S(1)}, u32[]{:S(2)}, u32[]{:S(2)}) async-start(bf16[4,8,48,256]{3,2,1,0:T(8,128)(2,1)} %pad_maximum_fusion.3), calls=%async_computation.3 | async-start | bytes 1572864 | tf_op jit(solution)/shard_map/all_to_all | solution.py:295
  387.5 10.8 %copy-start.5 = (bf16[4,8,48,256]{3,2,1,0:T(8,128)(2,1)}, bf16[4,8,48,256]{3,2,1,0:T(8,128)(2,1)S(1)}, u32[]{:S(2)}) copy-start(bf16[4,8,48,256]{3,2,1,0:T(8,128)(2,1)S(1)} %all-to-all-done.3) | copy-start | bytes 2359300
  388.6 19.0 %collective-permute-start = (bf16[16,48,256]{2,1,0:T(8,128)(2,1)}, bf16[16,48,256]{2,1,0:T(8,128)(2,1)S(1)}, u32[]{:S(2)}, u32[]{:S(2)}) collective-permute-start(bf16[16,48,256]{2,1,0:T(8,128)(2,1)} %bitcast.11), channel_id=1, source_target_pairs={{0,1},{1,2},{2,3},{3,4},{4,5},{5,6},{6,7},{8,9},{9,10},{10,11},{11... | collective-permute-start | bytes 1179656 | tf_op jit(solution)/shard_map/ppermute | solution.py:22
  390.5 17.1 %collective-permute-start.1 = (bf16[16,48,256]{2,1,0:T(8,128)(2,1)}, bf16[16,48,256]{2,1,0:T(8,128)(2,1)}, u32[]{:S(2)}, u32[]{:S(2)}) collective-permute-start(bf16[16,48,256]{2,1,0:T(8,128)(2,1)} %bitcast.13), channel_id=1, source_target_pairs={{1,0},{2,1},{3,2},{4,3},{5,4},{6,5},{7,6},{9,8},{10,9},{11,10},{12... | collective-permute-start | bytes 1179656 | tf_op jit(solution)/shard_map/ppermute | solution.py:25
  407.5 1.8 copy-start.6
where the time goes:
time: 420 us; the launch traced here: 419 us
  waiting for transfers between devices  193 us (46%)
  Pallas kernels  155 us (37%)
  local copies, waits for them, and re-layouts  29.9 us (7%)
  starting transfers between devices  25.2 us (6%)
  matrix products  9.6 us (2%)
  other arithmetic  6.53 us (2%)
    all_to_all x3, waiting for transfers between devices, body(): lax.all_to_all(arranged, ('wide', 'narrow'), split_axis=0, concat_axis=0,...  173 us
    pallas_call x3, Pallas kernels, channelize(): pl.pallas_call(channelize_kernel, grid=(inputs_here // group,), in_specs=...  102 us
    pallas_call x3, Pallas kernels, beam_power(): pl.pallas_call(beam_kernel, grid=(per_device,), in_specs=[pl.BlockSpec((s...  52.4 us
    all_to_all x1, waiting for transfers between devices, body(): lax.all_to_all(intensity, 'wide', split_axis=0, concat_axis=0, tiled=True)  19.7 us
    unnamed x16, local copies, waits for them, and re-layouts  17.8 us
    all_to_all x3, starting transfers between devices, body(): lax.all_to_all(arranged, ('wide', 'narrow'), split_axis=0, concat_axis=0,...  15.2 us
  transfers between devices with their start and end apart: 6, of which 4 were waited for; matrix products, arithmetic and copies ran while one was open for 3% of the time, Pallas kernels for 25%

commit v1 on v0

v1 whole, which is shorter than its diff:
```python
import dataclasses
import functools

import jax
import jax.numpy as jnp
from jax import lax
from jax.experimental import pallas as pl
from jax.experimental.pallas import tpu as pltpu
from jax.sharding import PartitionSpec as P

INTEG = 8
LANES = 128
BAND = 8
SLOTS = 3
LAG = 2
MESH = pl.DeviceIdType.MESH


@dataclasses.dataclass(frozen=True)
class Plan:
    wide: int
    narrow: int
    inputs: int
    per_device: int
    points: int
    taps: int
    pols: int
    dishes: int
    beams: int
    spectra: int

    @property
    def devices(self):
        return self.wide * self.narrow

    @property
    def groups(self):
        return max(1, self.inputs // 16)

    @property
    def rows(self):
        return self.inputs // self.groups

    @property
    def span(self):
        return LANES // (2 * self.groups)

    @property
    def chunks(self):
        return self.spectra // self.span

    @property
    def bins(self):
        return self.span // INTEG

    @property
    def halves(self):
        return self.points // LANES

    @property
    def tiles(self):
        return (self.span + self.taps - 1) * self.halves

    @property
    def per_pol(self):
        return self.devices // self.pols


def with_halo(block, sides, width):
    for axis, dim in sides:
        count = lax.axis_size(axis)
        forward = [(i, i + 1) for i in range(count - 1)]
        backward = [(target, source) for source, target in forward]
        low = lax.ppermute(
            lax.slice_in_dim(block, block.shape[dim] - width, None, axis=dim), axis, forward
        )
        high = lax.ppermute(lax.slice_in_dim(block, 0, width, axis=dim), axis, backward)
        block = jnp.concatenate([low, block, high], axis=dim)
    return block


def fourier_rows(points, owner_of):
    column = jnp.arange(points, dtype=jnp.int32)
    channel = owner_of(column)
    phase_index = channel[:, None] * column[None, :] % points
    angles = phase_index.astype(jnp.float32) * jnp.float32(2.0 * jnp.pi / points)
    scale = jnp.float32(1.0 / points**0.5)
    cosine = jnp.cos(angles) * scale
    sine_part = jnp.sin(angles) * scale
    real_row = jnp.concatenate([cosine, sine_part], axis=1)
    imag_row = jnp.concatenate([-sine_part, cosine], axis=1)
    return jnp.concatenate([real_row, imag_row], axis=0)


def split(value):
    high = value.astype(jnp.bfloat16)
    return high, (value - high.astype(jnp.float32)).astype(jnp.bfloat16)


def fused_kernel(
    plan,
    taps_ref,
    table_ref,
    samples_ref,
    weights_ref,
    recv_ref,
    intensity_ref,
    high_ref,
    low_ref,
    raw_ref,
    window_ref,
    stage_ref,
    send_ref,
    weight_ref,
    land_ref,
    energy_ref,
    raw_sem,
    weight_sem,
    send_sem,
    recv_sem,
    land_sem,
):
    span, rows, groups, halves = plan.span, plan.rows, plan.groups, plan.halves
    tap_count, points, chunks = plan.taps, plan.points, plan.chunks
    my_wide = lax.axis_index("wide")
    my_narrow = lax.axis_index("narrow")
    me = my_wide * plan.narrow + my_narrow

    def peer(step):
        return (
            lax.rem(my_wide + step // plan.narrow, plan.wide),
            lax.rem(my_narrow + step % plan.narrow, plan.narrow),
        )

    def load_raw(chunk, slot):
        @pl.loop(0, plan.tiles)
        def _(tile):
            column = pl.multiple_of((chunk * span * halves + tile) * LANES, LANES)
            pltpu.make_async_copy(
                samples_ref.at[:, :, pl.ds(column, LANES)], raw_ref.at[slot, tile], raw_sem.at[slot]
            ).start()

    barrier = pltpu.get_barrier_semaphore()
    load_raw(0, 0)

    @pl.loop(1, plan.devices)
    def _(step):
        pl.semaphore_signal(barrier, inc=1, device_id=peer(step), device_id_type=MESH)

    @pl.loop(0, plan.per_device)
    def _(channel):
        pltpu.make_async_copy(
            weights_ref.at[channel], weight_ref.at[channel], weight_sem
        ).start()

    high_ref[...], low_ref[...] = split(table_ref[...])

    def filter_rows(slot):
        row_groups = 2 * plan.inputs // 8

        @pl.loop(0, halves * row_groups)
        def _(index):
            half = index // row_groups
            group = index % row_groups
            coeffs = [
                jnp.broadcast_to(taps_ref[half, tap : tap + 1, :], (8, LANES))
                for tap in range(tap_count)
            ]
            sums = {}
            for frame in range(span + tap_count - 1):
                piece = raw_ref[slot, frame * halves + half, pl.ds(group * 4, 4)]
                value = piece.reshape(8, LANES).astype(jnp.float32)
                for out in range(max(0, frame - tap_count + 1), min(span - 1, frame) + 1):
                    term = coeffs[frame - out] * value
                    sums[out] = sums[out] + term if out in sums else term
                done = frame - tap_count + 1
                if done >= 0:
                    base = group * (8 * span) + done
                    window_ref[half, pl.ds(base, 8, stride=span), :] = sums.pop(done)

    def transform(slot):
        lane = lax.broadcasted_iota(jnp.int32, (points, LANES), 1)
        first = lane % (2 * span) < span
        product = functools.partial(
            lax.dot_general,
            dimension_numbers=(((1,), (1,)), ((), ())),
            preferred_element_type=jnp.float32,
        )
        pairs = 2

        @pl.loop(0, rows // (2 * pairs))
        def _(step):
            pieces = []
            for pair in range(pairs):
                for group in range(groups):
                    for member in range(2):
                        source = group * rows + step * (2 * pairs) + 2 * pair + member
                        blocks = []
                        for part in range(2):
                            start = pl.multiple_of((2 * source + part) * span, span)
                            for half in range(halves):
                                blocks.append(window_ref[half, pl.ds(start, span), :])
                        pieces.append(jnp.concatenate(blocks, axis=1))
            high, low = split(jnp.concatenate(pieces, axis=0))
            result = (
                product(low_ref[...], high)
                + product(high_ref[...], low)
                + product(high_ref[...], high)
            )
            for pair in range(pairs):
                real = result[:points, pair * LANES : (pair + 1) * LANES]
                imag = result[points:, pair * LANES : (pair + 1) * LANES]
                row = step * (2 * pairs) + 2 * pair
                stage_ref[pl.ds(row, points, stride=rows), :] = jnp.where(
                    first, real, pltpu.roll(imag, span, 1)
                )
                stage_ref[pl.ds(row + 1, points, stride=rows), :] = jnp.where(
                    first, pltpu.roll(real, LANES - span, 1), imag
                )

        send_ref[slot] = stage_ref[...].reshape(points, rows, LANES).astype(jnp.bfloat16)

    def start_sends(chunk, slot):
        @pl.loop(1, plan.devices)
        def _(step):
            wide, narrow = peer(step)
            target = wide * plan.narrow + narrow
            pltpu.make_async_remote_copy(
                src_ref=send_ref.at[slot, pl.ds(target * plan.per_device, plan.per_device)],
                dst_ref=recv_ref.at[chunk, me],
                send_sem=send_sem.at[slot],
                recv_sem=recv_sem.at[chunk],
                device_id=(wide, narrow),
                device_id_type=MESH,
            ).start()

        pltpu.make_async_copy(
            send_ref.at[slot, pl.ds(me * plan.per_device, plan.per_device)],
            recv_ref.at[chunk, me],
            recv_sem.at[chunk],
        ).start()

    def wait_sends(slot):
        sent = send_ref.at[slot, pl.ds(0, (plan.devices - 1) * plan.per_device)]
        pltpu.make_async_copy(sent, sent, send_sem.at[slot]).wait()

    def form_beams(chunk):
        arrived = recv_ref.at[chunk]
        pltpu.make_async_copy(arrived, arrived, recv_sem.at[chunk]).wait()
        landing = pltpu.make_async_copy(arrived, land_ref, land_sem)
        landing.start()
        landing.wait()
        together = 8 // plan.bins

        @pl.loop(0, plan.per_device // together)
        def _(step):
            binned = []
            for member in range(together):
                channel = step * together + member
                energy = None
                for pol in range(plan.pols):
                    block = land_ref[pol * plan.per_pol : (pol + 1) * plan.per_pol, channel]
                    block = block.astype(jnp.float32).reshape(plan.per_pol * rows, LANES)
                    turned = block.T.astype(jnp.bfloat16)
                    formed = None
                    for group in range(groups):
                        base = 2 * span * group
                        straight = turned[base : base + 2 * span]
                        crossed = jnp.concatenate(
                            [-straight[span:], straight[:span]], axis=0
                        )
                        for side, left in enumerate((straight, crossed)):
                            right = weight_ref[channel, pol, side, :, group]
                            right = right.reshape(-1, plan.beams)
                            term = jnp.dot(left, right, preferred_element_type=jnp.float32)
                            formed = term if formed is None else formed + term
                    squares = formed * formed
                    power = squares[:span] + squares[span:]
                    energy = power if energy is None else energy + power
                binned.append(energy.reshape(plan.bins, INTEG, plan.beams).sum(axis=1))
            energy_ref[pl.ds(pl.multiple_of(step * 8, 8), 8), :] = jnp.concatenate(
                binned, axis=0
            )

        scale = jnp.float32(1.0 / (plan.pols * INTEG))
        intensity_ref[chunk] = (energy_ref[...] * scale).astype(jnp.bfloat16)

    @pl.loop(0, chunks + LAG)
    def _(step):
        @pl.when(step < chunks)
        def _():
            side = step % 2
            slot = step % SLOTS
            raw = raw_ref.at[side]
            pltpu.make_async_copy(raw, raw, raw_sem.at[side]).wait()

            @pl.when(step + 1 < chunks)
            def _():
                load_raw(step + 1, 1 - side)

            filter_rows(side)

            @pl.when(step >= SLOTS)
            def _():
                wait_sends(slot)

            transform(slot)

            @pl.when(step == 0)
            def _():
                pl.semaphore_wait(barrier, plan.devices - 1)

            start_sends(step, slot)

        @pl.when(step == LAG)
        def _():
            pltpu.make_async_copy(weight_ref, weight_ref, weight_sem).wait()

        @pl.when(step >= LAG)
        def _():
            form_beams(step - LAG)

    for slot in range(min(SLOTS, chunks)):
        wait_sends(slot)


def fused(samples, filter_taps, table, beam_weights, plan):
    taps = filter_taps.reshape(plan.taps, plan.halves, LANES).transpose(1, 0, 2)
    if plan.groups == 1:
        dish_split = (1, 1, plan.dishes)
    else:
        dish_split = (plan.per_pol, plan.groups, plan.rows)
    weight_shape = (plan.per_device, plan.pols, 2, *dish_split, plan.beams)
    weights = beam_weights.reshape(weight_shape)
    anywhere = pl.BlockSpec(memory_space=pl.ANY)
    local = pl.BlockSpec(memory_space=pltpu.VMEM)
    recv_shape = (plan.chunks, plan.devices, plan.per_device, plan.rows, LANES)
    energy_shape = (plan.per_device * plan.bins, plan.beams)
    return pl.pallas_call(
        functools.partial(fused_kernel, plan),
        in_specs=[local, local, anywhere, anywhere],
        out_specs=[anywhere, local],
        out_shape=[
            jax.ShapeDtypeStruct(recv_shape, jnp.bfloat16),
            jax.ShapeDtypeStruct((plan.chunks, *energy_shape), jnp.bfloat16),
        ],
        scratch_shapes=[
            pltpu.VMEM(table.shape, jnp.bfloat16),
            pltpu.VMEM(table.shape, jnp.bfloat16),
            pltpu.VMEM((2, plan.tiles, plan.inputs, 2, LANES), jnp.bfloat16),
            pltpu.VMEM((plan.halves, 2 * plan.inputs * plan.span, LANES), jnp.float32),
            pltpu.VMEM((plan.points * plan.rows, LANES), jnp.float32),
            pltpu.VMEM((SLOTS, plan.points, plan.rows, LANES), jnp.bfloat16),
            pltpu.VMEM(weight_shape, jnp.bfloat16),
            pltpu.VMEM(recv_shape[1:], jnp.bfloat16),
            pltpu.VMEM(energy_shape, jnp.float32),
            pltpu.SemaphoreType.DMA((2,)),
            pltpu.SemaphoreType.DMA,
            pltpu.SemaphoreType.DMA((SLOTS,)),
            pltpu.SemaphoreType.DMA((plan.chunks,)),
            pltpu.SemaphoreType.DMA,
        ],
        compiler_params=pltpu.CompilerParams(
            collective_id=0, has_side_effects=True, vmem_limit_bytes=66 * 1000 * 1000
        ),
        name="fused",
    )(taps, table, samples, weights)[1]


def band_matrix(smooth_kernel, bin_count):
    extent = smooth_kernel.shape[0]
    half_width = extent // 2
    span = BAND + extent - 1
    offsets = jnp.arange(extent, dtype=jnp.int32)
    bins = jnp.arange(bin_count, dtype=jnp.int32)
    distance = bins[None, :] - bins[:, None] + half_width
    in_time = (distance[None] == offsets[:, None, None]).astype(jnp.float32)
    steps = jnp.arange(span, dtype=jnp.int32)[None, :] - jnp.arange(BAND, dtype=jnp.int32)[:, None]
    in_band = (steps[None] == offsets[:, None, None]).astype(jnp.float32)
    rows = jnp.einsum("kcj,kd->cjd", in_band, smooth_kernel, precision=lax.Precision.HIGHEST)
    matrix = jnp.einsum("cjd,dtu->ctju", rows, in_time, precision=lax.Precision.HIGHEST)
    return matrix.reshape(BAND * bin_count, span * bin_count)


def smooth(extended, matrix, half_width):
    channels_here = extended.shape[0] - 2 * half_width
    bin_count, beams = extended.shape[1:]
    values = extended.astype(jnp.float32)
    centered = values - jnp.mean(values, axis=1, keepdims=True)
    flat = centered.reshape(-1, beams)
    pieces = []
    for start in range(0, channels_here, BAND):
        rows = lax.slice_in_dim(flat, start * bin_count, start * bin_count + matrix.shape[1], axis=0)
        pieces.append(
            jnp.dot(
                matrix, rows, precision=lax.Precision.HIGH, preferred_element_type=jnp.float32
            )
        )
    return jnp.concatenate(pieces, axis=0).reshape(channels_here, bin_count, beams)


def body(samples, filter_taps, beam_weights, smooth_kernel):
    tap_count, points = filter_taps.shape
    wide_count = lax.axis_size("wide")
    narrow_count = lax.axis_size("narrow")
    per_device, pols, _, dishes, beams = beam_weights.shape
    frames = samples.shape[2] // points
    plan = Plan(
        wide=wide_count,
        narrow=narrow_count,
        inputs=samples.shape[0],
        per_device=per_device,
        points=points,
        taps=tap_count,
        pols=pols,
        dishes=dishes,
        beams=beams,
        spectra=frames - tap_count + 1,
    )

    def owner_of(column):
        device_slot = column // per_device
        return (
            device_slot % narrow_count * wide_count + device_slot // narrow_count
        ) * per_device + column % per_device

    table = fourier_rows(points, owner_of)
    matrix = band_matrix(smooth_kernel, plan.spectra // INTEG)
    pieces = fused(samples, filter_taps, table, beam_weights, plan)
    intensity = pieces.reshape(plan.chunks, per_device, plan.bins, wide_count, beams // wide_count)
    intensity = intensity.transpose(3, 1, 0, 2, 4)
    intensity = intensity.reshape(wide_count, per_device, -1, beams // wide_count)
    by_beam = lax.all_to_all(intensity, "wide", split_axis=0, concat_axis=0, tiled=True)
    by_beam = by_beam.reshape(-1, *by_beam.shape[2:])
    half_width = smooth_kernel.shape[0] // 2
    extended = with_halo(by_beam, (("narrow", 0),), half_width)
    return smooth(extended, matrix, half_width)


def solution(mesh):
    placed = (
        P(("wide", "narrow"), None, None),
        P(),
        P(("narrow", "wide"), None, None, None, None),
        P(),
    )
    return jax.shard_map(
        body, mesh=mesh, in_specs=placed, out_specs=P("narrow", None, "wide"), check_vma=False
    )
```

time: 420 us -> 361 us (0.86); the launches traced: 419 us -> 356 us
  waiting for transfers between devices: 193 us -> 20.5 us
  Pallas kernels: 155 us -> 289 us
  starting transfers between devices: 25.2 us -> 12.1 us
  local copies, waits for them, and re-layouts: 29.9 us -> 17.8 us
    all_to_all x3 -> x0, waiting for transfers between devices: 173 us -> none  [body(): lax.all_to_all(arranged, ('wide', 'narrow'), split_axis=0, concat_axis=0,...]
    pallas_call x6 -> x1, Pallas kernels: 155 us -> 289 us  [fused(): pl.pallas_call(functools.partial(fused_kernel, plan), in_specs=[local, lo...]
    unnamed x16 -> x6, local copies, waits for them, and re-layouts: 17.8 us -> 0.01 us
    all_to_all x3 -> x0, starting transfers between devices: 15.2 us -> none  [body(): lax.all_to_all(arranged, ('wide', 'narrow'), split_axis=0, concat_axis=0,...]
  transfers between devices with their start and end apart: 6 -> 3, of which waited for: 4 -> 1; matrix products, arithmetic and copies ran while one was open for 3% -> 4% of each run, Pallas kernels for 25% -> 0%
where the time goes in v1:
time: 361 us; the launch traced here: 356 us
  Pallas kernels  289 us (80%)
  waiting for transfers between devices  20.5 us (6%)
  local copies, waits for them, and re-layouts  17.8 us (5%)
  starting transfers between devices  12.1 us (3%)
  matrix products  9.6 us (3%)
  other arithmetic  6.19 us (2%)
    pallas_call x1, Pallas kernels, fused(): pl.pallas_call(functools.partial(fused_kernel, plan), in_specs=[local, lo...  289 us
    all_to_all x1, waiting for transfers between devices, body(): lax.all_to_all(intensity, 'wide', split_axis=0, concat_axis=0, tiled=True)  20.5 us
    all_to_all x1, starting transfers between devices, body(): lax.all_to_all(intensity, 'wide', split_axis=0, concat_axis=0, tiled=True)  7.56 us
  transfers between devices with their start and end apart: 3, of which 1 were waited for; matrix products, arithmetic and copies ran while one was open for 4% of the time, Pallas kernels for 0%

profile of v1, /device:TPU:4, one launch (start us, length us, event | category | flops | bytes accessed | tf_op | source)
XLA Modules:
  0.0 355.8 jit_solution(10043695917571629638)
XLA Ops:
  0.0 1.3 bitcast_bitcast_fusion.taps_ref
  1.3 1.1 sine_multiply_fusion
  2.5 1.1 maximum_maximum_fusion.table_ref
  3.5 289.4 %fused.1 = (bf16[12,32,8,16,128]{4,3,2,1,0:T(8,128)(2,1)}, bf16[12,32,1024]{2,1,0:T(8,128)(2,1)}) custom-call(f32[2,16,128]{2,1,0:T(8,128)} %bitcast_bitcast_fusion.taps_ref, f32[512,512]{1,0:T(8,128)} %maximum_maximum_fusion.table_ref, bf16[32,2,102144]{2,1,0:T(2,128)(2,1)} %samples_ref.1, bf16[8,2,2,16,2,16,1024]{6,5,4,3,2,1,0:T(8,128)(2,1)} %bitcast.42), custom_call_target="tpu_custom_call" | custom-call | tf_op jit(solution)/shard_map/fused/pallas_call | solution.py:339
  293.0 2.0 reshape.110
  295.0 1.1 copy.10
  296.1 7.6 %all-to-all-start = ((bf16[4,8,48,256]{3,1,2,0:T(8,128)(2,1)}), bf16[4,8,48,256]{3,1,2,0:T(8,128)(2,1)S(1)}, u32[]{:S(2)}, u32[]{:S(2)}) async-start(bf16[4,8,48,256]{3,1,2,0:T(8,128)(2,1)} %bitcast.8), calls=%async_computation | async-start | bytes 1572864 | tf_op jit(solution)/shard_map/all_to_all | solution.py:433
  304.0 20.5 %all-to-all-done = bf16[4,8,48,256]{3,1,2,0:T(8,128)(2,1)S(1)} async-done(((bf16[4,8,48,256]{3,1,2,0:T(8,128)(2,1)}), bf16[4,8,48,256]{3,1,2,0:T(8,128)(2,1)S(1)}, u32[]{:S(2)}, u32[]{:S(2)}) %all-to-all-start) | async-done | bytes 786464 | tf_op jit(solution)/shard_map/all_to_all | solution.py:433
  324.5 1.0 copy.11
  325.5 0.9 copy.13
  326.3 1.9 collective-permute-start.1
  328.3 2.6 collective-permute-start
  330.9 3.3 convolution_bitcast_fusion
  334.1 3.6 %copy.8 = f32[8,48,40,48]{3,2,1,0:T(8,128)} copy(f32[8,48,40,48]{3,2,0,1:T(8,128)S(1)} %convolution_bitcast_fusion) | data formatting | bytes 5898240 | tf_op jit(solution)/shard_map/cjd,dtu->ctju/transpose | solution.py:381
  337.7 5.7 %reshape.107 = f32[384,1920]{1,0:T(8,128)S(1)} reshape(f32[8,48,40,48]{3,2,1,0:T(8,128)} %copy.8) | data formatting | bytes 5898240 | tf_op jit(solution)/shard_map/reshape | solution.py:382
  343.4 1.3 copy.12
  344.7 1.4 convert_reduce_fusion
  346.1 1.3 convert_subtract_fusion
  347.4 1.0 fusion.17
  348.4 1.5 fusion.19
  349.9 1.5 fusion.22
  351.5 1.5 fusion.21
  353.0 1.5 fusion.20
  354.5 1.2 pad_maximum_fusion.1
  (14 shorter events, 0.4 us)
Async XLA Ops:
  0.0 303.7 %copy-start = (f32[33,33]{1,0:T(8,128)S(1)}, f32[33,33]{1,0:T(8,128)}, u32[]{:S(2)}) copy-start(f32[33,33]{1,0:T(8,128)} %param.7) | copy-start | bytes 13072
  296.1 28.4 %all-to-all-start = ((bf16[4,8,48,256]{3,1,2,0:T(8,128)(2,1)}), bf16[4,8,48,256]{3,1,2,0:T(8,128)(2,1)S(1)}, u32[]{:S(2)}, u32[]{:S(2)}) async-start(bf16[4,8,48,256]{3,1,2,0:T(8,128)(2,1)} %bitcast.8), calls=%async_computation | async-start | bytes 1572864 | tf_op jit(solution)/shard_map/all_to_all | solution.py:433
  324.5 9.7 %copy-start.2 = (bf16[4,8,48,256]{3,1,2,0:T(8,128)(2,1)}, bf16[4,8,48,256]{3,1,2,0:T(8,128)(2,1)S(1)}, u32[]{:S(2)}) copy-start(bf16[4,8,48,256]{3,1,2,0:T(8,128)(2,1)S(1)} %all-to-all-done) | copy-start | bytes 2359300
  326.3 18.3 %collective-permute-start.1 = (bf16[16,48,256]{2,1,0:T(8,128)(2,1)}, bf16[16,48,256]{2,1,0:T(8,128)(2,1)S(1)}, u32[]{:S(2)}, u32[]{:S(2)}) collective-permute-start(bf16[16,48,256]{2,1,0:T(8,128)(2,1)} %bitcast.11), channel_id=1, source_target_pairs={{1,0},{2,1},{3,2},{4,3},{5,4},{6,5},{7,6},{9,8},{10,9},{11,10},{12... | collective-permute-start | bytes 1179656 | tf_op jit(solution)/shard_map/ppermute | solution.py:77
  328.3 16.4 %collective-permute-start = (bf16[16,48,256]{2,1,0:T(8,128)(2,1)}, bf16[16,48,256]{2,1,0:T(8,128)(2,1)}, u32[]{:S(2)}, u32[]{:S(2)}) collective-permute-start(bf16[16,48,256]{2,1,0:T(8,128)(2,1)} %bitcast.9), channel_id=1, source_target_pairs={{0,1},{1,2},{2,3},{3,4},{4,5},{5,6},{6,7},{8,9},{9,10},{10,11},{11... | collective-permute-start | bytes 1179656 | tf_op jit(solution)/shard_map/ppermute | solution.py:74
  353.0 2.8 copy-start.1

commit v2 on v1

--- a/solution.py
+++ b/solution.py
@@ -3,6 +3,7 @@
 
 import jax
 import jax.numpy as jnp
+import numpy as np
 from jax import lax
 from jax.experimental import pallas as pl
 from jax.experimental.pallas import tpu as pltpu
@@ -13,6 +14,8 @@
 BAND = 8
 SLOTS = 3
 LAG = 2
+HALO_LAG = 4
+SMOOTH_LAG = 5
 MESH = pl.DeviceIdType.MESH
 
 
@@ -28,6 +31,7 @@
     dishes: int
     beams: int
     spectra: int
+    extent: int
 
     @property
     def devices(self):
@@ -65,31 +69,62 @@
     def per_pol(self):
         return self.devices // self.pols
 
-
-def with_halo(block, sides, width):
-    for axis, dim in sides:
-        count = lax.axis_size(axis)
-        forward = [(i, i + 1) for i in range(count - 1)]
-        backward = [(target, source) for source, target in forward]
-        low = lax.ppermute(
-            lax.slice_in_dim(block, block.shape[dim] - width, None, axis=dim), axis, forward
-        )
-        high = lax.ppermute(lax.slice_in_dim(block, 0, width, axis=dim), axis, backward)
-        block = jnp.concatenate([low, block, high], axis=dim)
-    return block
+    @property
+    def half(self):
+        return self.extent // 2
+
+    @property
+    def share(self):
+        return self.beams // self.wide
+
+    @property
+    def local(self):
+        return self.wide * self.per_device
+
+    @property
+    def all_bins(self):
+        return self.spectra // INTEG
+
+    @property
+    def reach(self):
+        return (BAND + self.extent - 1) * self.bins
+
+    @property
+    def lanes(self):
+        return -(-self.reach // LANES) * LANES
+
+    @property
+    def shifts(self):
+        return -(-(2 * self.all_bins - self.bins) // 8) * 8
 
 
 def fourier_rows(points, owner_of):
-    column = jnp.arange(points, dtype=jnp.int32)
-    channel = owner_of(column)
-    phase_index = channel[:, None] * column[None, :] % points
-    angles = phase_index.astype(jnp.float32) * jnp.float32(2.0 * jnp.pi / points)
-    scale = jnp.float32(1.0 / points**0.5)
-    cosine = jnp.cos(angles) * scale
-    sine_part = jnp.sin(angles) * scale
-    real_row = jnp.concatenate([cosine, sine_part], axis=1)
-    imag_row = jnp.concatenate([-sine_part, cosine], axis=1)
-    return jnp.concatenate([real_row, imag_row], axis=0)
+    column = np.arange(points)
+    phase_index = owner_of(column)[:, None] * column[None, :] % points
+    angles = phase_index * (2.0 * np.pi / points)
+    cosine = np.cos(angles) / np.sqrt(points)
+    sine_part = np.sin(angles) / np.sqrt(points)
+    real_row = np.concatenate([cosine, sine_part], axis=1)
+    imag_row = np.concatenate([-sine_part, cosine], axis=1)
+    table = np.concatenate([real_row, imag_row], axis=0).astype(np.float32)
+    high = table.astype(jnp.bfloat16)
+    return np.stack([high, (table - high.astype(np.float32)).astype(jnp.bfloat16)])
+
+
+def one_hot(shape, matches):
+    row = lax.broadcasted_iota(jnp.int32, shape, 0)
+    column = lax.broadcasted_iota(jnp.int32, shape, 1)
+    return matches(row, column).astype(jnp.float32)
+
+
+def exact_dot(left, right, contract=(1, 0)):
+    return lax.dot_general(
+        left,
+        right,
+        (((contract[0],), (contract[1],)), ((), ())),
+        precision=lax.Precision.HIGHEST,
+        preferred_element_type=jnp.float32,
+    )
 
 
 def split(value):
@@ -100,13 +135,13 @@
 def fused_kernel(
     plan,
     taps_ref,
-    table_ref,
+    smooth_ref,
+    table_hbm,
     samples_ref,
     weights_ref,
     recv_ref,
-    intensity_ref,
-    high_ref,
-    low_ref,
+    out_ref,
+    table_ref,
     raw_ref,
     window_ref,
     stage_ref,
@@ -114,11 +149,22 @@
     weight_ref,
     land_ref,
     energy_ref,
+    shifted_ref,
+    matrix_ref,
+    outgoing_ref,
+    gather_ref,
     raw_sem,
+    table_sem,
     weight_sem,
     send_sem,
     recv_sem,
     land_sem,
+    share_sem,
+    gather_sem,
+    up_sem,
+    down_sem,
+    low_sem,
+    high_sem,
 ):
     span, rows, groups, halves = plan.span, plan.rows, plan.groups, plan.halves
     tap_count, points, chunks = plan.taps, plan.points, plan.chunks
@@ -140,8 +186,13 @@
                 samples_ref.at[:, :, pl.ds(column, LANES)], raw_ref.at[slot, tile], raw_sem.at[slot]
             ).start()
 
+    own_start = plan.half * plan.bins
+    own_rows = plan.local * plan.bins
+    part_rows = plan.per_device * plan.bins
+
     barrier = pltpu.get_barrier_semaphore()
     load_raw(0, 0)
+    pltpu.make_async_copy(table_hbm, table_ref, table_sem).start()
 
     @pl.loop(1, plan.devices)
     def _(step):
@@ -153,7 +204,20 @@
             weights_ref.at[channel], weight_ref.at[channel], weight_sem
         ).start()
 
-    high_ref[...], low_ref[...] = split(table_ref[...])
+    out_ref[...] = jnp.zeros_like(out_ref)
+
+    def clear(start):
+        gather_ref[:, start : start + own_start] = jnp.zeros(
+            (chunks, own_start, plan.share), jnp.bfloat16
+        )
+
+    @pl.when(my_narrow == 0)
+    def _():
+        clear(0)
+
+    @pl.when(my_narrow == plan.narrow - 1)
+    def _():
+        clear(own_start + own_rows)
 
     def filter_rows(slot):
         row_groups = 2 * plan.inputs // 8
@@ -162,8 +226,9 @@
         def _(index):
             half = index // row_groups
             group = index % row_groups
+            columns = pl.ds(pl.multiple_of(half * LANES, LANES), LANES)
             coeffs = [
-                jnp.broadcast_to(taps_ref[half, tap : tap + 1, :], (8, LANES))
+                jnp.broadcast_to(taps_ref[tap : tap + 1, columns], (8, LANES))
                 for tap in range(tap_count)
             ]
             sums = {}
@@ -203,9 +268,9 @@
                         pieces.append(jnp.concatenate(blocks, axis=1))
             high, low = split(jnp.concatenate(pieces, axis=0))
             result = (
-                product(low_ref[...], high)
-                + product(high_ref[...], low)
-                + product(high_ref[...], high)
+                product(table_ref[1], high)
+                + product(table_ref[0], low)
+                + product(table_ref[0], high)
             )
             for pair in range(pairs):
                 real = result[:points, pair * LANES : (pair + 1) * LANES]
@@ -283,9 +348,124 @@
             )
 
         scale = jnp.float32(1.0 / (plan.pols * INTEG))
-        intensity_ref[chunk] = (energy_ref[...] * scale).astype(jnp.bfloat16)
-
-    @pl.loop(0, chunks + LAG)
+        intensity = (energy_ref[...] * scale).astype(jnp.bfloat16)
+        for owner in range(plan.wide):
+            outgoing_ref[chunk, owner] = intensity[:, owner * plan.share : (owner + 1) * plan.share]
+
+        mine = pl.ds(pl.multiple_of(own_start + my_wide * part_rows, part_rows), part_rows)
+
+        @pl.loop(1, plan.wide)
+        def _(step):
+            target = lax.rem(my_wide + step, plan.wide)
+            pltpu.make_async_remote_copy(
+                src_ref=outgoing_ref.at[chunk, target],
+                dst_ref=gather_ref.at[chunk, mine],
+                send_sem=share_sem.at[chunk],
+                recv_sem=gather_sem.at[chunk],
+                device_id=(target, my_narrow),
+                device_id_type=MESH,
+            ).start()
+
+        pltpu.make_async_copy(
+            outgoing_ref.at[chunk, my_wide], gather_ref.at[chunk, mine], gather_sem.at[chunk]
+        ).start()
+
+    def halo(chunk):
+        def upward():
+            return pltpu.make_async_remote_copy(
+                src_ref=gather_ref.at[chunk, pl.ds(own_rows, own_start)],
+                dst_ref=gather_ref.at[chunk, pl.ds(0, own_start)],
+                send_sem=up_sem.at[chunk],
+                recv_sem=low_sem.at[chunk],
+                device_id=(my_wide, my_narrow + 1),
+                device_id_type=MESH,
+            )
+
+        def downward():
+            return pltpu.make_async_remote_copy(
+                src_ref=gather_ref.at[chunk, pl.ds(own_start, own_start)],
+                dst_ref=gather_ref.at[chunk, pl.ds(own_start + own_rows, own_start)],
+                send_sem=down_sem.at[chunk],
+                recv_sem=high_sem.at[chunk],
+                device_id=(my_wide, my_narrow - 1),
+                device_id_type=MESH,
+            )
+
+        return upward, downward
+
+    def start_halo(chunk):
+        own = gather_ref.at[chunk, pl.ds(own_start, own_rows)]
+        pltpu.make_async_copy(own, own, gather_sem.at[chunk]).wait()
+        upward, downward = halo(chunk)
+
+        @pl.when(my_narrow < plan.narrow - 1)
+        def _():
+            upward().start()
+
+        @pl.when(my_narrow > 0)
+        def _():
+            downward().start()
+
+    def build_matrix():
+        extent, bins, shifts, lanes = plan.extent, plan.bins, plan.shifts, plan.lanes
+        last = plan.all_bins - bins
+        spread = one_hot((extent, lanes), lambda row, column: row == column // bins)
+        columns = exact_dot(smooth_ref[...], spread, (0, 0))
+        inner = lax.broadcasted_iota(jnp.int32, (shifts, lanes), 1) % bins
+        shifted = jnp.zeros((shifts, lanes), jnp.float32)
+        for offset in range(bins):
+            select = one_hot(
+                (shifts, extent),
+                lambda row, column: column == offset - row + last + plan.half,
+            )
+            shifted = jnp.where(inner == offset, exact_dot(select, columns), shifted)
+        shifted_ref[...] = shifted
+        gather = one_hot(
+            (plan.all_bins, shifts),
+            lambda row, column: (column >= row)
+            & (column <= row + last)
+            & ((column - row) % bins == 0),
+        )
+        block = one_hot((lanes, lanes), lambda row, column: row // bins == column // bins)
+        total = exact_dot(exact_dot(gather, shifted), block)
+        mean = total * jnp.float32(1.0 / plan.all_bins)
+
+        @pl.loop(0, chunks)
+        def _(chunk):
+            start = shifts - (last - bins * chunk)
+            rows_here = pltpu.roll(shifted_ref[...], lax.rem(start, shifts), 0)[: plan.all_bins]
+            centered = rows_here - mean
+            for channel in range(BAND):
+                moved = pltpu.roll(centered, bins * channel, 1) if channel else centered
+                place = slice(channel * plan.all_bins, (channel + 1) * plan.all_bins)
+                matrix_ref[chunk, 0, place], matrix_ref[chunk, 1, place] = split(moved)
+
+    def smooth(chunk):
+        upward, downward = halo(chunk)
+
+        @pl.when(my_narrow > 0)
+        def _():
+            upward().wait_recv()
+
+        @pl.when(my_narrow < plan.narrow - 1)
+        def _():
+            downward().wait_recv()
+
+        for band in range(plan.local // BAND):
+            start = band * BAND * plan.bins
+            values = gather_ref[chunk, start : start + plan.reach]
+            size = BAND * plan.all_bins
+            place = slice(band * size, (band + 1) * size)
+            total = out_ref[place]
+            for side in (1, 0):
+                total = total + jnp.dot(
+                    matrix_ref[chunk, side, :, : plan.reach],
+                    values,
+                    preferred_element_type=jnp.float32,
+                )
+            out_ref[place] = total
+
+    @pl.loop(0, chunks + SMOOTH_LAG)
     def _(step):
         @pl.when(step < chunks)
         def _():
@@ -304,6 +484,10 @@
             def _():
                 wait_sends(slot)
 
+            @pl.when(step == 0)
+            def _():
+                pltpu.make_async_copy(table_hbm, table_ref, table_sem).wait()
+
             transform(slot)
 
             @pl.when(step == 0)
@@ -314,18 +498,40 @@
 
         @pl.when(step == LAG)
         def _():
+            build_matrix()
             pltpu.make_async_copy(weight_ref, weight_ref, weight_sem).wait()
 
-        @pl.when(step >= LAG)
+        @pl.when((step >= LAG) & (step < chunks + LAG))
         def _():
             form_beams(step - LAG)
+
+        @pl.when((step >= HALO_LAG) & (step < chunks + HALO_LAG))
+        def _():
+            start_halo(step - HALO_LAG)
+
+        @pl.when(step >= SMOOTH_LAG)
+        def _():
+            smooth(step - SMOOTH_LAG)
 
     for slot in range(min(SLOTS, chunks)):
         wait_sends(slot)
 
-
-def fused(samples, filter_taps, table, beam_weights, plan):
-    taps = filter_taps.reshape(plan.taps, plan.halves, LANES).transpose(1, 0, 2)
+    @pl.loop(0, chunks)
+    def _(chunk):
+        sent = outgoing_ref.at[chunk, pl.ds(0, plan.wide - 1)]
+        pltpu.make_async_copy(sent, sent, share_sem.at[chunk]).wait()
+        upward, downward = halo(chunk)
+
+        @pl.when(my_narrow < plan.narrow - 1)
+        def _():
+            upward().wait_send()
+
+        @pl.when(my_narrow > 0)
+        def _():
+            downward().wait_send()
+
+
+def fused(samples, filter_taps, table, beam_weights, smooth_kernel, plan):
     if plan.groups == 1:
         dish_split = (1, 1, plan.dishes)
     else:
@@ -336,16 +542,18 @@
     local = pl.BlockSpec(memory_space=pltpu.VMEM)
     recv_shape = (plan.chunks, plan.devices, plan.per_device, plan.rows, LANES)
     energy_shape = (plan.per_device * plan.bins, plan.beams)
+    ext_rows = (plan.local + 2 * plan.half) * plan.bins
+    out_shape = (plan.local * plan.all_bins, plan.share)
+    per_chunk = pltpu.SemaphoreType.DMA((plan.chunks,))
     return pl.pallas_call(
         functools.partial(fused_kernel, plan),
-        in_specs=[local, local, anywhere, anywhere],
+        in_specs=[local, local, anywhere, anywhere, anywhere],
         out_specs=[anywhere, local],
         out_shape=[
             jax.ShapeDtypeStruct(recv_shape, jnp.bfloat16),
-            jax.ShapeDtypeStruct((plan.chunks, *energy_shape), jnp.bfloat16),
+            jax.ShapeDtypeStruct(out_shape, jnp.float32),
         ],
         scratch_shapes=[
-            pltpu.VMEM(table.shape, jnp.bfloat16),
             pltpu.VMEM(table.shape, jnp.bfloat16),
             pltpu.VMEM((2, plan.tiles, plan.inputs, 2, LANES), jnp.bfloat16),
             pltpu.VMEM((plan.halves, 2 * plan.inputs * plan.span, LANES), jnp.float32),
@@ -354,49 +562,25 @@
             pltpu.VMEM(weight_shape, jnp.bfloat16),
             pltpu.VMEM(recv_shape[1:], jnp.bfloat16),
             pltpu.VMEM(energy_shape, jnp.float32),
+            pltpu.VMEM((plan.shifts, plan.lanes), jnp.float32),
+            pltpu.VMEM((plan.chunks, 2, BAND * plan.all_bins, plan.lanes), jnp.bfloat16),
+            pltpu.VMEM(
+                (plan.chunks, plan.wide, plan.per_device * plan.bins, plan.share), jnp.bfloat16
+            ),
+            pltpu.VMEM((plan.chunks, ext_rows, plan.share), jnp.bfloat16),
             pltpu.SemaphoreType.DMA((2,)),
             pltpu.SemaphoreType.DMA,
+            pltpu.SemaphoreType.DMA,
             pltpu.SemaphoreType.DMA((SLOTS,)),
-            pltpu.SemaphoreType.DMA((plan.chunks,)),
+            per_chunk,
             pltpu.SemaphoreType.DMA,
+            *([per_chunk] * 6),
         ],
         compiler_params=pltpu.CompilerParams(
             collective_id=0, has_side_effects=True, vmem_limit_bytes=66 * 1000 * 1000
         ),
         name="fused",
-    )(taps, table, samples, weights)[1]
-
-
-def band_matrix(smooth_kernel, bin_count):
-    extent = smooth_kernel.shape[0]
-    half_width = extent // 2
-    span = BAND + extent - 1
-    offsets = jnp.arange(extent, dtype=jnp.int32)
-    bins = jnp.arange(bin_count, dtype=jnp.int32)
-    distance = bins[None, :] - bins[:, None] + half_width
-    in_time = (distance[None] == offsets[:, None, None]).astype(jnp.float32)
-    steps = jnp.arange(span, dtype=jnp.int32)[None, :] - jnp.arange(BAND, dtype=jnp.int32)[:, None]
-    in_band = (steps[None] == offsets[:, None, None]).astype(jnp.float32)
-    rows = jnp.einsum("kcj,kd->cjd", in_band, smooth_kernel, precision=lax.Precision.HIGHEST)
-    matrix = jnp.einsum("cjd,dtu->ctju", rows, in_time, precision=lax.Precision.HIGHEST)
-    return matrix.reshape(BAND * bin_count, span * bin_count)
-
-
-def smooth(extended, matrix, half_width):
-    channels_here = extended.shape[0] - 2 * half_width
-    bin_count, beams = extended.shape[1:]
-    values = extended.astype(jnp.float32)
-    centered = values - jnp.mean(values, axis=1, keepdims=True)
-    flat = centered.reshape(-1, beams)
-    pieces = []
-    for start in range(0, channels_here, BAND):
-        rows = lax.slice_in_dim(flat, start * bin_count, start * bin_count + matrix.shape[1], axis=0)
-        pieces.append(
-            jnp.dot(
-                matrix, rows, precision=lax.Precision.HIGH, preferred_element_type=jnp.float32
-            )
-        )
-    return jnp.concatenate(pieces, axis=0).reshape(channels_here, bin_count, beams)
+    )(filter_taps, smooth_kernel, table, samples, weights)[1]
 
 
 def body(samples, filter_taps, beam_weights, smooth_kernel):
@@ -416,6 +600,7 @@
         dishes=dishes,
         beams=beams,
         spectra=frames - tap_count + 1,
+        extent=smooth_kernel.shape[0],
     )
 
     def owner_of(column):
@@ -424,17 +609,9 @@
             device_slot % narrow_count * wide_count + device_slot // narrow_count
         ) * per_device + column % per_device
 
-    table = fourier_rows(points, owner_of)
-    matrix = band_matrix(smooth_kernel, plan.spectra // INTEG)
-    pieces = fused(samples, filter_taps, table, beam_weights, plan)
-    intensity = pieces.reshape(plan.chunks, per_device, plan.bins, wide_count, beams // wide_count)
-    intensity = intensity.transpose(3, 1, 0, 2, 4)
-    intensity = intensity.reshape(wide_count, per_device, -1, beams // wide_count)
-    by_beam = lax.all_to_all(intensity, "wide", split_axis=0, concat_axis=0, tiled=True)
-    by_beam = by_beam.reshape(-1, *by_beam.shape[2:])
-    half_width = smooth_kernel.shape[0] // 2
-    extended = with_halo(by_beam, (("narrow", 0),), half_width)
-    return smooth(extended, matrix, half_width)
+    table = jnp.asarray(fourier_rows(points, owner_of))
+    filtered = fused(samples, filter_taps, table, beam_weights, smooth_kernel, plan)
+    return filtered.reshape(plan.local, plan.all_bins, plan.share)
 
 
 def solution(mesh):

time: 361 us -> 320 us (0.89)
  Pallas kernels: 289 us -> 315 us
  waiting for transfers between devices: 20.5 us -> 0 us
  local copies, waits for them, and re-layouts: 17.8 us -> 2.66 us
  starting transfers between devices: 12.1 us -> 0 us
  matrix products: 9.6 us -> 0 us
  other arithmetic: 6.19 us -> 0 us
    pallas_call x1, Pallas kernels: 289 us -> 315 us  [fused(): pl.pallas_call(functools.partial(fused_kernel, plan), in_specs=[local, lo...]
    all_to_all x1 -> x0, waiting for transfers between devices: 20.5 us -> none  [body(): lax.all_to_all(intensity, 'wide', split_axis=0, concat_axis=0, tiled=True)]
    dot_general x6 -> x0, matrix products: 9.6 us -> none  [the longest x4 6.06 us: smooth(): jnp.dot(matrix, rows, precision=lax.Precision.HIGH, preferred_element_typ...]
    reshape x3 -> x0, local copies, waits for them, and re-layouts: 8.75 us -> none  [the longest x1 5.66 us: band_matrix(): return matrix.reshape(BAND * bin_count, span * bin_count)]
    all_to_all x1 -> x0, starting transfers between devices: 7.56 us -> none  [body(): lax.all_to_all(intensity, 'wide', split_axis=0, concat_axis=0, tiled=True)]
    transpose x2 -> x0, local copies, waits for them, and re-layouts: 4.88 us -> none  [the longest x1 3.56 us: band_matrix(): jnp.einsum('cjd,dtu->ctju', rows, in_time, precision=lax.Precision.HIGHEST)]
    ppermute x2 -> x0, starting transfers between devices: 4.5 us -> none  [the longest x1 2.59 us: with_halo(): lax.ppermute(lax.slice_in_dim(block, block.shape[dim] - width, None, axis...]
  transfers between devices with their start and end apart: 3 -> 0, of which waited for: 1 -> 0; matrix products, arithmetic and copies ran while one was open for 4% -> 0% of each run, Pallas kernels for 0% -> 0%
where the time goes in v2:
time: 320 us; the launch traced here: 317 us
  Pallas kernels  315 us (98%)
    pallas_call x1, Pallas kernels, fused(): pl.pallas_call(functools.partial(fused_kernel, plan), in_specs=[local, lo...  315 us

profile of v2, /device:TPU:4, one launch (start us, length us, event | category | flops | bytes accessed | tf_op | source)
XLA Modules:
  0.0 317.4 jit_solution(6820626605263363581)
XLA Ops:
  0.0 314.7 %fused.1 = (bf16[12,32,8,16,128]{4,3,2,1,0:T(8,128)(2,1)}, f32[1536,256]{1,0:T(8,128)}) custom-call(f32[16,256]{1,0:T(8,128)} %taps_ref.1, f32[33,33]{1,0:T(8,128)} %smooth_ref.1, bf16[2,512,512]{2,1,0:T(8,128)(2,1)} %constant.2.clone.table_hbm, bf16[32,2,102144]{2,1,0:T(2,128)(2,1)} %samples_ref.1, bf16[8,2,2,16,2,16,1024]{6,5,4,3,2,1,0:T(8,128)(2,1)} %bitcast.2), custom_call_target="tpu_custom_call" | custom-call | tf_op jit(solution)/shard_map/fused/pallas_call | solution.py:548
  314.7 2.7 copy.7

commit v3 on v2

--- a/solution.py
+++ b/solution.py
@@ -56,6 +56,14 @@
     @property
     def bins(self):
         return self.span // INTEG
+
+    @property
+    def together(self):
+        return 8 // self.bins
+
+    @property
+    def sets(self):
+        return self.per_device // self.together
 
     @property
     def halves(self):
@@ -158,6 +166,7 @@
     weight_sem,
     send_sem,
     recv_sem,
+    last_sem,
     land_sem,
     share_sem,
     gather_sem,
@@ -186,6 +195,7 @@
                 samples_ref.at[:, :, pl.ds(column, LANES)], raw_ref.at[slot, tile], raw_sem.at[slot]
             ).start()
 
+    last = chunks - 1
     own_start = plan.half * plan.bins
     own_rows = plan.local * plan.bins
     part_rows = plan.per_device * plan.bins
@@ -305,26 +315,60 @@
             recv_sem.at[chunk],
         ).start()
 
+    def start_last(index, slot):
+        def voltages(target):
+            first = target * plan.per_device + index * plan.together
+            return send_ref.at[slot, pl.ds(first, plan.together)]
+
+        landing = land_ref.at[1, me, pl.ds(index * plan.together, plan.together)]
+
+        @pl.loop(1, plan.devices)
+        def _(step):
+            wide, narrow = peer(step)
+            pltpu.make_async_remote_copy(
+                src_ref=voltages(wide * plan.narrow + narrow),
+                dst_ref=landing,
+                send_sem=send_sem.at[slot],
+                recv_sem=last_sem.at[index],
+                device_id=(wide, narrow),
+                device_id_type=MESH,
+            ).start()
+
+        pltpu.make_async_copy(voltages(me), landing, last_sem.at[index]).start()
+
     def wait_sends(slot):
         sent = send_ref.at[slot, pl.ds(0, (plan.devices - 1) * plan.per_device)]
         pltpu.make_async_copy(sent, sent, send_sem.at[slot]).wait()
 
     def form_beams(chunk):
-        arrived = recv_ref.at[chunk]
-        pltpu.make_async_copy(arrived, arrived, recv_sem.at[chunk]).wait()
-        landing = pltpu.make_async_copy(arrived, land_ref, land_sem)
-        landing.start()
-        landing.wait()
-        together = 8 // plan.bins
-
-        @pl.loop(0, plan.per_device // together)
+        together = plan.together
+        landed = (chunk == last).astype(jnp.int32)
+
+        @pl.when(chunk < last)
+        def _():
+            arrived = recv_ref.at[chunk]
+            pltpu.make_async_copy(arrived, arrived, recv_sem.at[chunk]).wait()
+            landing = pltpu.make_async_copy(arrived, land_ref.at[0], land_sem)
+            landing.start()
+            landing.wait()
+
+        @pl.loop(0, plan.sets)
         def _(step):
+            @pl.when((chunk == last) & (step == plan.sets - 1))
+            def _():
+                catch_up()
+
+            @pl.when(chunk == last)
+            def _():
+                arrived = land_ref.at[1, :, pl.ds(step * together, together)]
+                pltpu.make_async_copy(arrived, arrived, last_sem.at[step]).wait()
+
             binned = []
             for member in range(together):
                 channel = step * together + member
                 energy = None
                 for pol in range(plan.pols):
-                    block = land_ref[pol * plan.per_pol : (pol + 1) * plan.per_pol, channel]
+                    block = land_ref[landed, pol * plan.per_pol : (pol + 1) * plan.per_pol, channel]
                     block = block.astype(jnp.float32).reshape(plan.per_pol * rows, LANES)
                     turned = block.T.astype(jnp.bfloat16)
                     formed = None
@@ -465,7 +509,13 @@
                 )
             out_ref[place] = total
 
-    @pl.loop(0, chunks + SMOOTH_LAG)
+    def catch_up():
+        start_halo(last - 2)
+        smooth(last - 3)
+        start_halo(last - 1)
+        smooth(last - 2)
+
+    @pl.loop(0, chunks + LAG)
     def _(step):
         @pl.when(step < chunks)
         def _():
@@ -494,24 +544,40 @@
             def _():
                 pl.semaphore_wait(barrier, plan.devices - 1)
 
-            start_sends(step, slot)
+            @pl.when(step < last)
+            def _():
+                start_sends(step, slot)
+
+            @pl.when(step == last)
+            def _():
+                @pl.loop(0, plan.sets - 1)
+                def _(index):
+                    start_last(index, slot)
 
         @pl.when(step == LAG)
         def _():
             build_matrix()
             pltpu.make_async_copy(weight_ref, weight_ref, weight_sem).wait()
 
-        @pl.when((step >= LAG) & (step < chunks + LAG))
+        @pl.when(step >= LAG)
         def _():
             form_beams(step - LAG)
 
-        @pl.when((step >= HALO_LAG) & (step < chunks + HALO_LAG))
+        @pl.when(step == last + 1)
+        def _():
+            start_last(plan.sets - 1, last % SLOTS)
+
+        @pl.when((step >= HALO_LAG) & (step <= last + 1))
         def _():
             start_halo(step - HALO_LAG)
 
-        @pl.when(step >= SMOOTH_LAG)
+        @pl.when((step >= SMOOTH_LAG) & (step <= last + 1))
         def _():
             smooth(step - SMOOTH_LAG)
+
+    smooth(last - 1)
+    start_halo(last)
+    smooth(last)
 
     for slot in range(min(SLOTS, chunks)):
         wait_sends(slot)
@@ -540,7 +606,7 @@
     weights = beam_weights.reshape(weight_shape)
     anywhere = pl.BlockSpec(memory_space=pl.ANY)
     local = pl.BlockSpec(memory_space=pltpu.VMEM)
-    recv_shape = (plan.chunks, plan.devices, plan.per_device, plan.rows, LANES)
+    recv_shape = (plan.chunks - 1, plan.devices, plan.per_device, plan.rows, LANES)
     energy_shape = (plan.per_device * plan.bins, plan.beams)
     ext_rows = (plan.local + 2 * plan.half) * plan.bins
     out_shape = (plan.local * plan.all_bins, plan.share)
@@ -560,7 +626,7 @@
             pltpu.VMEM((plan.points * plan.rows, LANES), jnp.float32),
             pltpu.VMEM((SLOTS, plan.points, plan.rows, LANES), jnp.bfloat16),
             pltpu.VMEM(weight_shape, jnp.bfloat16),
-            pltpu.VMEM(recv_shape[1:], jnp.bfloat16),
+            pltpu.VMEM((2, *recv_shape[1:]), jnp.bfloat16),
             pltpu.VMEM(energy_shape, jnp.float32),
             pltpu.VMEM((plan.shifts, plan.lanes), jnp.float32),
             pltpu.VMEM((plan.chunks, 2, BAND * plan.all_bins, plan.lanes), jnp.bfloat16),
@@ -573,6 +639,7 @@
             pltpu.SemaphoreType.DMA,
             pltpu.SemaphoreType.DMA((SLOTS,)),
             per_chunk,
+            pltpu.SemaphoreType.DMA((plan.sets,)),
             pltpu.SemaphoreType.DMA,
             *([per_chunk] * 6),
         ],

time: 320 us -> 319 us (level)
  no operation moved by 1% of the time
where the time goes in v3:
time: 319 us; the launch traced here: 317 us
  Pallas kernels  314 us (98%)
    pallas_call x1, Pallas kernels, fused(): pl.pallas_call(functools.partial(fused_kernel, plan), in_specs=[local, lo...  314 us

profile of v3, /device:TPU:4, one launch (start us, length us, event | category | flops | bytes accessed | tf_op | source)
XLA Modules:
  0.0 317.0 jit_solution(13963928628069283023)
XLA Ops:
  0.0 314.4 %fused.1 = (bf16[11,32,8,16,128]{4,3,2,1,0:T(8,128)(2,1)}, f32[1536,256]{1,0:T(8,128)}) custom-call(f32[16,256]{1,0:T(8,128)} %taps_ref.1, f32[33,33]{1,0:T(8,128)} %smooth_ref.1, bf16[2,512,512]{2,1,0:T(8,128)(2,1)} %constant.2.clone.table_hbm, bf16[32,2,102144]{2,1,0:T(2,128)(2,1)} %samples_ref.1, bf16[8,2,2,16,2,16,1024]{6,5,4,3,2,1,0:T(8,128)(2,1)} %bitcast.2), custom_call_target="tpu_custom_call" | custom-call | tf_op jit(solution)/shard_map/fused/pallas_call | solution.py:614
  314.4 2.7 copy.7

commit v4 on v3

--- a/solution.py
+++ b/solution.py
@@ -14,6 +14,7 @@
 BAND = 8
 SLOTS = 3
 LAG = 2
+PAIRS = 2
 HALO_LAG = 4
 SMOOTH_LAG = 5
 MESH = pl.DeviceIdType.MESH
@@ -58,6 +59,10 @@
         return self.span // INTEG
 
     @property
+    def turns(self):
+        return self.rows // (2 * PAIRS)
+
+    @property
     def together(self):
         return 8 // self.bins
 
@@ -106,7 +111,7 @@
         return -(-(2 * self.all_bins - self.bins) // 8) * 8
 
 
-def fourier_rows(points, owner_of):
+def fourier_rows(points, owner_of, blocks):
     column = np.arange(points)
     phase_index = owner_of(column)[:, None] * column[None, :] % points
     angles = phase_index * (2.0 * np.pi / points)
@@ -114,7 +119,8 @@
     sine_part = np.sin(angles) / np.sqrt(points)
     real_row = np.concatenate([cosine, sine_part], axis=1)
     imag_row = np.concatenate([-sine_part, cosine], axis=1)
-    table = np.concatenate([real_row, imag_row], axis=0).astype(np.float32)
+    table = np.stack([part.reshape(blocks, -1, 2 * points) for part in (real_row, imag_row)], axis=1)
+    table = table.reshape(2 * points, 2 * points).astype(np.float32)
     high = table.astype(jnp.bfloat16)
     return np.stack([high, (table - high.astype(np.float32)).astype(jnp.bfloat16)])
 
@@ -152,6 +158,7 @@
     table_ref,
     raw_ref,
     window_ref,
+    signal_ref,
     stage_ref,
     send_ref,
     weight_ref,
@@ -253,67 +260,84 @@
                     base = group * (8 * span) + done
                     window_ref[half, pl.ds(base, 8, stride=span), :] = sums.pop(done)
 
-    def transform(slot):
-        lane = lax.broadcasted_iota(jnp.int32, (points, LANES), 1)
+    def prepare():
+        @pl.loop(0, plan.turns)
+        def _(step):
+            pieces = []
+            for pair in range(PAIRS):
+                for group in range(groups):
+                    for member in range(2):
+                        source = group * rows + step * (2 * PAIRS) + 2 * pair + member
+                        blocks = []
+                        for part in range(2):
+                            start = pl.multiple_of((2 * source + part) * span, span)
+                            for half in range(halves):
+                                blocks.append(window_ref[half, pl.ds(start, span), :])
+                        pieces.append(jnp.concatenate(blocks, axis=1))
+            signal_ref[0, step], signal_ref[1, step] = split(jnp.concatenate(pieces, axis=0))
+
+    def transform(block, slot):
+        channels = plan.narrow * plan.per_device
+        lane = lax.broadcasted_iota(jnp.int32, (channels, LANES), 1)
         first = lane % (2 * span) < span
         product = functools.partial(
             lax.dot_general,
             dimension_numbers=(((1,), (1,)), ((), ())),
             preferred_element_type=jnp.float32,
         )
-        pairs = 2
-
-        @pl.loop(0, rows // (2 * pairs))
+        table_rows = pl.ds(pl.multiple_of(block * (2 * channels), 2 * channels), 2 * channels)
+
+        @pl.loop(0, plan.turns)
         def _(step):
-            pieces = []
-            for pair in range(pairs):
-                for group in range(groups):
-                    for member in range(2):
-                        source = group * rows + step * (2 * pairs) + 2 * pair + member
-                        blocks = []
-                        for part in range(2):
-                            start = pl.multiple_of((2 * source + part) * span, span)
-                            for half in range(halves):
-                                blocks.append(window_ref[half, pl.ds(start, span), :])
-                        pieces.append(jnp.concatenate(blocks, axis=1))
-            high, low = split(jnp.concatenate(pieces, axis=0))
+            high, low = signal_ref[0, step], signal_ref[1, step]
             result = (
-                product(table_ref[1], high)
-                + product(table_ref[0], low)
-                + product(table_ref[0], high)
+                product(table_ref[1, table_rows], high)
+                + product(table_ref[0, table_rows], low)
+                + product(table_ref[0, table_rows], high)
             )
-            for pair in range(pairs):
-                real = result[:points, pair * LANES : (pair + 1) * LANES]
-                imag = result[points:, pair * LANES : (pair + 1) * LANES]
-                row = step * (2 * pairs) + 2 * pair
-                stage_ref[pl.ds(row, points, stride=rows), :] = jnp.where(
+            for pair in range(PAIRS):
+                real = result[:channels, pair * LANES : (pair + 1) * LANES]
+                imag = result[channels:, pair * LANES : (pair + 1) * LANES]
+                row = step * (2 * PAIRS) + 2 * pair
+                stage_ref[pl.ds(row, channels, stride=rows), :] = jnp.where(
                     first, real, pltpu.roll(imag, span, 1)
                 )
-                stage_ref[pl.ds(row + 1, points, stride=rows), :] = jnp.where(
+                stage_ref[pl.ds(row + 1, channels, stride=rows), :] = jnp.where(
                     first, pltpu.roll(real, LANES - span, 1), imag
                 )
 
-        send_ref[slot] = stage_ref[...].reshape(points, rows, LANES).astype(jnp.bfloat16)
-
-    def start_sends(chunk, slot):
-        @pl.loop(1, plan.devices)
+        place = pl.ds(pl.multiple_of(block * channels, channels), channels)
+        send_ref[slot, place] = (
+            stage_ref[...].reshape(channels, rows, LANES).astype(jnp.bfloat16)
+        )
+
+    def block_at(step):
+        moved = lax.rem(step + plan.wide // 2, plan.wide)
+        if plan.wide & (plan.wide - 1) == 0:
+            return lax.bitwise_xor(my_wide, moved)
+        return lax.rem(my_wide + moved, plan.wide)
+
+    def start_sends(chunk, block, slot):
+        @pl.loop(0, plan.narrow)
         def _(step):
-            wide, narrow = peer(step)
-            target = wide * plan.narrow + narrow
-            pltpu.make_async_remote_copy(
-                src_ref=send_ref.at[slot, pl.ds(target * plan.per_device, plan.per_device)],
-                dst_ref=recv_ref.at[chunk, me],
-                send_sem=send_sem.at[slot],
-                recv_sem=recv_sem.at[chunk],
-                device_id=(wide, narrow),
-                device_id_type=MESH,
-            ).start()
-
-        pltpu.make_async_copy(
-            send_ref.at[slot, pl.ds(me * plan.per_device, plan.per_device)],
-            recv_ref.at[chunk, me],
-            recv_sem.at[chunk],
-        ).start()
+            narrow = lax.rem(my_narrow + step, plan.narrow)
+            target = block * plan.narrow + narrow
+            source = send_ref.at[slot, pl.ds(target * plan.per_device, plan.per_device)]
+
+            @pl.when(target != me)
+            def _():
+                pltpu.make_async_remote_copy(
+                    src_ref=source,
+                    dst_ref=recv_ref.at[chunk, me],
+                    send_sem=send_sem.at[slot],
+                    recv_sem=recv_sem.at[chunk],
+                    device_id=(block, narrow),
+                    device_id_type=MESH,
+                ).start()
+
+            @pl.when(target == me)
+            def _():
+                pltpu.make_async_copy(source, recv_ref.at[chunk, me], recv_sem.at[chunk]).start()
 
     def start_last(index, slot):
         def voltages(target):
@@ -538,15 +562,20 @@
             def _():
                 pltpu.make_async_copy(table_hbm, table_ref, table_sem).wait()
 
-            transform(slot)
-
-            @pl.when(step == 0)
-            def _():
-                pl.semaphore_wait(barrier, plan.devices - 1)
-
-            @pl.when(step < last)
-            def _():
-                start_sends(step, slot)
+            prepare()
+
+            @pl.loop(0, plan.wide)
+            def _(turn):
+                block = block_at(turn)
+                transform(block, slot)
+
+                @pl.when((step == 0) & (turn == 0))
+                def _():
+                    pl.semaphore_wait(barrier, plan.devices - 1)
+
+                @pl.when(step < last)
+                def _():
+                    start_sends(step, block, slot)
 
             @pl.when(step == last)
             def _():
@@ -617,13 +646,14 @@
         out_specs=[anywhere, local],
         out_shape=[
             jax.ShapeDtypeStruct(recv_shape, jnp.bfloat16),
-            jax.ShapeDtypeStruct(out_shape, jnp.float32),
+            pltpu.VMEM(out_shape, jnp.float32),
         ],
         scratch_shapes=[
             pltpu.VMEM(table.shape, jnp.bfloat16),
             pltpu.VMEM((2, plan.tiles, plan.inputs, 2, LANES), jnp.bfloat16),
             pltpu.VMEM((plan.halves, 2 * plan.inputs * plan.span, LANES), jnp.float32),
-            pltpu.VMEM((plan.points * plan.rows, LANES), jnp.float32),
+            pltpu.VMEM((2, plan.turns, 2 * PAIRS * plan.groups * plan.span, 2 * plan.points), jnp.bfloat16),
+            pltpu.VMEM((plan.points // plan.wide * plan.rows, LANES), jnp.float32),
             pltpu.VMEM((SLOTS, plan.points, plan.rows, LANES), jnp.bfloat16),
             pltpu.VMEM(weight_shape, jnp.bfloat16),
             pltpu.VMEM((2, *recv_shape[1:]), jnp.bfloat16),
@@ -644,7 +674,7 @@
             *([per_chunk] * 6),
         ],
         compiler_params=pltpu.CompilerParams(
-            collective_id=0, has_side_effects=True, vmem_limit_bytes=66 * 1000 * 1000
+            collective_id=0, has_side_effects=True, vmem_limit_bytes=62 * 1000 * 1000
         ),
         name="fused",
     )(filter_taps, smooth_kernel, table, samples, weights)[1]
@@ -676,7 +706,7 @@
             device_slot % narrow_count * wide_count + device_slot // narrow_count
         ) * per_device + column % per_device
 
-    table = jnp.asarray(fourier_rows(points, owner_of))
+    table = jnp.asarray(fourier_rows(points, owner_of, wide_count))
     filtered = fused(samples, filter_taps, table, beam_weights, smooth_kernel, plan)
     return filtered.reshape(plan.local, plan.all_bins, plan.share)
 

time: 319 us -> 312 us (0.978)
  Pallas kernels: 314 us -> 309 us
    pallas_call x1, Pallas kernels: 314 us -> 309 us  [fused(): pl.pallas_call(functools.partial(fused_kernel, plan), in_specs=[local, lo...]
where the time goes in v4:
time: 312 us; the launch traced here: 310 us
  Pallas kernels  309 us (99%)
    pallas_call x1, Pallas kernels, fused(): pl.pallas_call(functools.partial(fused_kernel, plan), in_specs=[local, lo...  309 us

profile of v4, /device:TPU:4, one launch (start us, length us, event | category | flops | bytes accessed | tf_op | source)
XLA Modules:
  0.0 310.4 jit_solution(9017915996842922911)
XLA Ops:
  0.0 309.2 %fused.1 = (bf16[11,32,8,16,128]{4,3,2,1,0:T(8,128)(2,1)}, f32[1536,256]{1,0:T(8,128)S(1)}) custom-call(f32[16,256]{1,0:T(8,128)} %taps_ref.1, f32[33,33]{1,0:T(8,128)} %smooth_ref.1, bf16[2,512,512]{2,1,0:T(8,128)(2,1)} %constant.2.clone.table_hbm, bf16[32,2,102144]{2,1,0:T(2,128)(2,1)} %samples_ref.1, bf16[8,2,2,16,2,16,1024]{6,5,4,3,2,1,0:T(8,128)(2,1)} %bitcast.3), custom_call_target="tpu_custom_call" | custom-call | tf_op jit(solution)/shard_map/fused/pallas_call | solution.py:643
  309.2 1.1 copy.7

commit v5 on v4

--- a/solution.py
+++ b/solution.py
@@ -208,12 +208,13 @@
     part_rows = plan.per_device * plan.bins
 
     barrier = pltpu.get_barrier_semaphore()
-    load_raw(0, 0)
-    pltpu.make_async_copy(table_hbm, table_ref, table_sem).start()
 
     @pl.loop(1, plan.devices)
     def _(step):
         pl.semaphore_signal(barrier, inc=1, device_id=peer(step), device_id_type=MESH)
+
+    load_raw(0, 0)
+    pltpu.make_async_copy(table_hbm, table_ref, table_sem).start()
 
     @pl.loop(0, plan.per_device)
     def _(channel):
@@ -378,6 +379,18 @@
 
         @pl.loop(0, plan.sets)
         def _(step):
+            if plan.sets > 2:
+
+                @pl.when((chunk == last - 1) & (step == 0))
+                def _():
+                    start_last(plan.sets - 2, last % SLOTS)
+
+            if plan.sets > 1:
+
+                @pl.when((chunk == last - 1) & (step == plan.sets - 1))
+                def _():
+                    start_last(plan.sets - 1, last % SLOTS)
+
             @pl.when((chunk == last) & (step == plan.sets - 1))
             def _():
                 catch_up()
@@ -536,7 +549,6 @@
     def catch_up():
         start_halo(last - 2)
         smooth(last - 3)
-        start_halo(last - 1)
         smooth(last - 2)
 
     @pl.loop(0, chunks + LAG)
@@ -579,7 +591,7 @@
 
             @pl.when(step == last)
             def _():
-                @pl.loop(0, plan.sets - 1)
+                @pl.loop(0, max(1, plan.sets - 2))
                 def _(index):
                     start_last(index, slot)
 
@@ -592,10 +604,6 @@
         def _():
             form_beams(step - LAG)
 
-        @pl.when(step == last + 1)
-        def _():
-            start_last(plan.sets - 1, last % SLOTS)
-
         @pl.when((step >= HALO_LAG) & (step <= last + 1))
         def _():
             start_halo(step - HALO_LAG)
@@ -604,6 +612,7 @@
         def _():
             smooth(step - SMOOTH_LAG)
 
+    start_halo(last - 1)
     smooth(last - 1)
     start_halo(last)
     smooth(last)

time: 312 us -> 314 us (level)
  no operation moved by 1% of the time
where the time goes in v5:
time: 314 us; the launch traced here: 312 us
  Pallas kernels  311 us (99%)
    pallas_call x1, Pallas kernels, fused(): pl.pallas_call(functools.partial(fused_kernel, plan), in_specs=[local, lo...  311 us

profile of v5, /device:TPU:4, one launch (start us, length us, event | category | flops | bytes accessed | tf_op | source)
XLA Modules:
  0.0 312.2 jit_solution(3760341375280306734)
XLA Ops:
  0.0 311.1 %fused.1 = (bf16[11,32,8,16,128]{4,3,2,1,0:T(8,128)(2,1)}, f32[1536,256]{1,0:T(8,128)S(1)}) custom-call(f32[16,256]{1,0:T(8,128)} %taps_ref.1, f32[33,33]{1,0:T(8,128)} %smooth_ref.1, bf16[2,512,512]{2,1,0:T(8,128)(2,1)} %constant.2.clone.table_hbm, bf16[32,2,102144]{2,1,0:T(2,128)(2,1)} %samples_ref.1, bf16[8,2,2,16,2,16,1024]{6,5,4,3,2,1,0:T(8,128)(2,1)} %bitcast.3), custom_call_target="tpu_custom_call" | custom-call | tf_op jit(solution)/shard_map/fused/pallas_call | solution.py:652
  311.1 1.1 copy.7

commit v6 on v4

--- a/solution.py
+++ b/solution.py
@@ -12,9 +12,10 @@
 INTEG = 8
 LANES = 128
 BAND = 8
-SLOTS = 3
+SLOTS = 4
 LAG = 2
 PAIRS = 2
+HELD = 1
 HALO_LAG = 4
 SMOOTH_LAG = 5
 MESH = pl.DeviceIdType.MESH
@@ -250,8 +251,8 @@
             ]
             sums = {}
             for frame in range(span + tap_count - 1):
-                piece = raw_ref[slot, frame * halves + half, pl.ds(group * 4, 4)]
-                value = piece.reshape(8, LANES).astype(jnp.float32)
+                view = raw_ref.at[slot, frame * halves + half].reshape(2 * plan.inputs, LANES)
+                value = view[pl.ds(pl.multiple_of(group * 8, 8), 8)].astype(jnp.float32)
                 for out in range(max(0, frame - tap_count + 1), min(span - 1, frame) + 1):
                     term = coeffs[frame - out] * value
                     sums[out] = sums[out] + term if out in sums else term
@@ -364,6 +365,25 @@
         sent = send_ref.at[slot, pl.ds(0, (plan.devices - 1) * plan.per_device)]
         pltpu.make_async_copy(sent, sent, send_sem.at[slot]).wait()
 
+    def share_intensity(chunk):
+        mine = pl.ds(pl.multiple_of(own_start + my_wide * part_rows, part_rows), part_rows)
+
+        @pl.loop(1, plan.wide)
+        def _(step):
+            target = lax.rem(my_wide + step, plan.wide)
+            pltpu.make_async_remote_copy(
+                src_ref=outgoing_ref.at[chunk, target],
+                dst_ref=gather_ref.at[chunk, mine],
+                send_sem=share_sem.at[chunk],
+                recv_sem=gather_sem.at[chunk],
+                device_id=(target, my_narrow),
+                device_id_type=MESH,
+            ).start()
+
+        pltpu.make_async_copy(
+            outgoing_ref.at[chunk, my_wide], gather_ref.at[chunk, mine], gather_sem.at[chunk]
+        ).start()
+
     def form_beams(chunk):
         together = plan.together
         landed = (chunk == last).astype(jnp.int32)
@@ -386,6 +406,11 @@
             def _():
                 arrived = land_ref.at[1, :, pl.ds(step * together, together)]
                 pltpu.make_async_copy(arrived, arrived, last_sem.at[step]).wait()
+
+            @pl.when((chunk == last) & (step == plan.sets - 1))
+            def _():
+                for held in range(HELD, 0, -1):
+                    share_intensity(last - held)
 
             binned = []
             for member in range(together):
@@ -420,23 +445,9 @@
         for owner in range(plan.wide):
             outgoing_ref[chunk, owner] = intensity[:, owner * plan.share : (owner + 1) * plan.share]
 
-        mine = pl.ds(pl.multiple_of(own_start + my_wide * part_rows, part_rows), part_rows)
-
-        @pl.loop(1, plan.wide)
-        def _(step):
-            target = lax.rem(my_wide + step, plan.wide)
-            pltpu.make_async_remote_copy(
-                src_ref=outgoing_ref.at[chunk, target],
-                dst_ref=gather_ref.at[chunk, mine],
-                send_sem=share_sem.at[chunk],
-                recv_sem=gather_sem.at[chunk],
-                device_id=(target, my_narrow),
-                device_id_type=MESH,
-            ).start()
-
-        pltpu.make_async_copy(
-            outgoing_ref.at[chunk, my_wide], gather_ref.at[chunk, mine], gather_sem.at[chunk]
-        ).start()
+        @pl.when((chunk < last - HELD) | (chunk == last))
+        def _():
+            share_intensity(chunk)
 
     def halo(chunk):
         def upward():
@@ -536,8 +547,6 @@
     def catch_up():
         start_halo(last - 2)
         smooth(last - 3)
-        start_halo(last - 1)
-        smooth(last - 2)
 
     @pl.loop(0, chunks + LAG)
     def _(step):
@@ -604,6 +613,8 @@
         def _():
             smooth(step - SMOOTH_LAG)
 
+    start_halo(last - 1)
+    smooth(last - 2)
     smooth(last - 1)
     start_halo(last)
     smooth(last)

time: 312 us -> 310 us (level)
  no operation moved by 1% of the time
where the time goes in v6:
time: 310 us
  Pallas kernels  308 us (99%)
    pallas_call x1, Pallas kernels, fused(): pl.pallas_call(functools.partial(fused_kernel, plan), in_specs=[local, lo...  308 us

profile of v6, /device:TPU:4, one launch (start us, length us, event | category | flops | bytes accessed | tf_op | source)
XLA Modules:
  0.0 309.6 jit_solution(260268598409965239)
XLA Ops:
  0.0 308.4 %fused.1 = (bf16[11,32,8,16,128]{4,3,2,1,0:T(8,128)(2,1)}, f32[1536,256]{1,0:T(8,128)S(1)}) custom-call(f32[16,256]{1,0:T(8,128)} %taps_ref.1, f32[33,33]{1,0:T(8,128)} %smooth_ref.1, bf16[2,512,512]{2,1,0:T(8,128)(2,1)} %constant.2.clone.table_hbm, bf16[32,2,102144]{2,1,0:T(2,128)(2,1)} %samples_ref.1, bf16[8,2,2,16,2,16,1024]{6,5,4,3,2,1,0:T(8,128)(2,1)} %bitcast.3), custom_call_target="tpu_custom_call" | custom-call | tf_op jit(solution)/shard_map/fused/pallas_call | solution.py:654
  308.4 1.1 copy.7

commit v7 on v6

--- a/solution.py
+++ b/solution.py
@@ -216,26 +216,27 @@
     def _(step):
         pl.semaphore_signal(barrier, inc=1, device_id=peer(step), device_id_type=MESH)
 
-    @pl.loop(0, plan.per_device)
-    def _(channel):
-        pltpu.make_async_copy(
-            weights_ref.at[channel], weight_ref.at[channel], weight_sem
-        ).start()
-
-    out_ref[...] = jnp.zeros_like(out_ref)
-
-    def clear(start):
-        gather_ref[:, start : start + own_start] = jnp.zeros(
-            (chunks, own_start, plan.share), jnp.bfloat16
-        )
-
-    @pl.when(my_narrow == 0)
-    def _():
-        clear(0)
-
-    @pl.when(my_narrow == plan.narrow - 1)
-    def _():
-        clear(own_start + own_rows)
+    def set_up():
+        @pl.loop(0, plan.per_device)
+        def _(channel):
+            pltpu.make_async_copy(
+                weights_ref.at[channel], weight_ref.at[channel], weight_sem
+            ).start()
+
+        out_ref[...] = jnp.zeros_like(out_ref)
+
+        def clear(start):
+            gather_ref[:, start : start + own_start] = jnp.zeros(
+                (chunks, own_start, plan.share), jnp.bfloat16
+            )
+
+        @pl.when(my_narrow == 0)
+        def _():
+            clear(0)
+
+        @pl.when(my_narrow == plan.narrow - 1)
+        def _():
+            clear(own_start + own_rows)
 
     def filter_rows(slot):
         row_groups = 2 * plan.inputs // 8
@@ -251,8 +252,8 @@
             ]
             sums = {}
             for frame in range(span + tap_count - 1):
-                view = raw_ref.at[slot, frame * halves + half].reshape(2 * plan.inputs, LANES)
-                value = view[pl.ds(pl.multiple_of(group * 8, 8), 8)].astype(jnp.float32)
+                piece = raw_ref[slot, frame * halves + half, pl.ds(group * 4, 4)]
+                value = piece.reshape(8, LANES).astype(jnp.float32)
                 for out in range(max(0, frame - tap_count + 1), min(span - 1, frame) + 1):
                     term = coeffs[frame - out] * value
                     sums[out] = sums[out] + term if out in sums else term
@@ -313,7 +314,9 @@
         )
 
     def block_at(step):
-        moved = lax.rem(step + plan.wide // 2, plan.wide)
+        near = plan.wide - plan.wide // 2
+        moved = jnp.where(step < plan.wide // 2, step + near, step - plan.wide // 2 + 1)
+        moved = jnp.where(step == plan.wide - 1, 0, moved)
         if plan.wide & (plan.wide - 1) == 0:
             return lax.bitwise_xor(my_wide, moved)
         return lax.rem(my_wide + moved, plan.wide)
@@ -321,7 +324,10 @@
     def start_sends(chunk, block, slot):
         @pl.loop(0, plan.narrow)
         def _(step):
-            narrow = lax.rem(my_narrow + step, plan.narrow)
+            if plan.narrow & (plan.narrow - 1) == 0:
+                narrow = lax.bitwise_xor(my_narrow, step)
+            else:
+                narrow = lax.rem(my_narrow + step, plan.narrow)
             target = block * plan.narrow + narrow
             source = send_ref.at[slot, pl.ds(target * plan.per_device, plan.per_device)]
 
@@ -591,6 +597,10 @@
                 @pl.loop(0, plan.sets - 1)
                 def _(index):
                     start_last(index, slot)
+
+        @pl.when(step == 0)
+        def _():
+            set_up()
 
         @pl.when(step == LAG)
         def _():

time: 310 us -> 310 us (level)
  no operation moved by 1% of the time
where the time goes in v7:
time: 310 us
  Pallas kernels  308 us (99%)
    pallas_call x1, Pallas kernels, fused(): pl.pallas_call(functools.partial(fused_kernel, plan), in_specs=[local, lo...  308 us

profile of v7, /device:TPU:4, one launch (start us, length us, event | category | flops | bytes accessed | tf_op | source)
XLA Modules:
  0.0 309.5 jit_solution(6591523356488850672)
XLA Ops:
  0.0 308.3 %fused.1 = (bf16[11,32,8,16,128]{4,3,2,1,0:T(8,128)(2,1)}, f32[1536,256]{1,0:T(8,128)S(1)}) custom-call(f32[16,256]{1,0:T(8,128)} %taps_ref.1, f32[33,33]{1,0:T(8,128)} %smooth_ref.1, bf16[2,512,512]{2,1,0:T(8,128)(2,1)} %constant.2.clone.table_hbm, bf16[32,2,102144]{2,1,0:T(2,128)(2,1)} %samples_ref.1, bf16[8,2,2,16,2,16,1024]{6,5,4,3,2,1,0:T(8,128)(2,1)} %bitcast.3), custom_call_target="tpu_custom_call" | custom-call | tf_op jit(solution)/shard_map/fused/pallas_call | solution.py:664
  308.4 1.1 copy.7
